TPU v7x, 256 devices: a whole 4x4x8 slice. The times are simulated.
256 devices in a mesh: tensor: 8 (over y, core), store: 32 (over z, x).
Axes of the slice: x: 4, y: 4, z: 8, core: 2. Of those that a mesh axis runs over, the one named last changes fastest.
Arguments:
- inputs: bfloat16 [512, 16, 28672], P('tensor', None, 'store'), may hold values from -6 to 6
- out_grads: bfloat16 [512, 16, 8192], P('tensor', None, 'store'), may hold values from -6 to 6
- proj_in: bfloat16 [28672, 128], P('store'), may hold values from -0.03125 to 0.03125
- proj_out: bfloat16 [8192, 128], P('store'), may hold values from -0.125 to 0.125
- inv_fisher: float32 [16384, 16384], P('store', 'tensor'), may hold values from -1 to 4
- store_grads: float32 [8192, 16384], P('store', 'tensor'), may hold values from -0.005859375 to 0.005859375
Outputs:
- scores: float32 [512, 8192], P('tensor', 'store')
All inputs are finite; a program needn't handle non-finite values.
Results may differ from a plain program's by a relative error of at most 0.0003.
Values sent between devices are 32-bit elements; how exact they have to be, the bound alone decides.
No kernel may reach another device: no remote copies, remote signals or barrier semaphores. Data moves between devices by JAX's collectives and lax.ppermute only.
A program may use at most 64 MiB of HBM per device.

v0:
```python
import jax
import jax.numpy as jnp
from jax import lax
from jax.sharding import Mesh, PartitionSpec as P


HIGH = lax.Precision.HIGH
SWAP = [(0, 1), (1, 0)]


def shifted(array, axis, size, steps):
    if steps % size == 0:
        return array
    return lax.ppermute(array, axis, [(i, (i + steps) % size) for i in range(size)])


def summed_share(array, axis, size):
    pieces = lax.all_to_all(array.reshape(size, array.shape[0] // size, array.shape[1]), axis, 0, 0)
    return jnp.sum(pieces, axis=0)


def everyones(array, axis, size):
    copies = jnp.broadcast_to(array[None], (size,) + array.shape)
    gathered = lax.all_to_all(copies, axis, 0, 0)
    return gathered.reshape((size * array.shape[0],) + array.shape[1:])


def on_device(sizes, inputs, out_grads, proj_in, proj_out, inv_fisher, store_grads):
    ny, nz, nx = sizes["y"], sizes["z"], sizes["x"]
    examples, tokens = inputs.shape[0], inputs.shape[1]
    pj, pk = proj_in.shape[1], proj_out.shape[1]
    x = lax.axis_index("x")
    act_part = jnp.dot(inputs.reshape(examples * tokens, -1), proj_in, preferred_element_type=jnp.float32)
    grad_part = jnp.dot(out_grads.reshape(examples * tokens, -1), proj_out, preferred_element_type=jnp.float32)

    width = inv_fisher.shape[1] // nx

    def spread(array):
        own, other = [], []
        for k in range(nx):
            piece = lax.dynamic_slice_in_dim(array, ((x + k) & (nx - 1)) * width, width, 1)
            piece = shifted(piece, "x", nx, k)
            own.append(piece)
            other.append(lax.ppermute(piece, "core", SWAP))
        return own, other

    fisher = spread(inv_fisher)
    stored = spread(store_grads)

    both = jnp.concatenate([act_part, grad_part], axis=1)
    both = summed_share(both, "x", nx)
    both = summed_share(both, "z", nz)
    few = examples // (nx * nz)
    act = both[:, :pj].reshape(few, tokens, pj)
    grad = both[:, pj:].reshape(few, tokens, pk)
    local = jnp.einsum("etk,etj->ekj", grad, act, precision=lax.Precision.HIGHEST)
    local = local.reshape(few, nz, -1).transpose(1, 0, 2)
    coords = local.shape[2]
    mine = lax.all_to_all(local, "z", 0, 0).reshape(few * nz, coords)
    mine = everyones(mine, "x", nx)
    rows = coords // nx
    mine = jnp.concatenate(
        [lax.dynamic_slice_in_dim(mine, ((x - k) & (nx - 1)) * rows, rows, 1) for k in range(nx)], axis=1
    )
    owned = []
    for d in range(ny):
        owned.append(shifted(mine, "y", ny, -d))
    these = jnp.concatenate(owned, axis=0)
    part = []
    for blocks in fisher:
        total = None
        for k in range(nx):
            term = jnp.dot(
                these[:, k * rows : (k + 1) * rows], blocks[k], precision=HIGH, preferred_element_type=jnp.float32
            )
            total = term if total is None else total + term
        part.append(total)
    part = jnp.concatenate(part, axis=1)
    whole = everyones(summed_share(part, "z", nz), "z", nz)
    summed = None
    for k in range(nx):
        scored = None
        for side, blocks in enumerate(stored):
            term = lax.dot_general(
                whole[:, side * width : (side + 1) * width],
                blocks[k],
                (((1,), (1,)), ((), ())),
                precision=HIGH,
                preferred_element_type=jnp.float32,
            )
            scored = term if scored is None else scored + term
        back = shifted(scored, "x", nx, -k)
        summed = back if summed is None else summed + back
    result = None
    for d in range(ny):
        home = shifted(summed[d * examples : (d + 1) * examples], "y", ny, d)
        result = home if result is None else result + home
    return result


def solution(mesh):
    sizes = {"y": 4, "core": 2, "z": 8, "x": 4}
    named = Mesh(mesh.devices.reshape(tuple(sizes.values())), tuple(sizes))
    tensor, store = ("y", "core"), ("z", "x")
    placed = (
        P(tensor, None, store),
        P(tensor, None, store),
        P(store, None),
        P(store, None),
        P(store, tensor),
        P(store, tensor),
    )

    def run(*args):
        return on_device(sizes, *args)

    return jax.shard_map(run, mesh=named, in_specs=placed, out_specs=P(tensor, store), check_vma=False)
```

profile of v0, /device:TPU:6, one launch (start us, length us, event | category | flops | bytes accessed | tf_op | source)
XLA Modules:
  0.0 215.7 jit_solution(9846133834447617152)
XLA Ops:
  3.7 17.6 %all_to_all.30 = f32[4,256,256]{1,2,0:T(8,128)S(1)} all-to-all(f32[4,256,256]{1,2,0:T(8,128)S(1)} %bitcast.48), channel_id=1, replica_groups=mesh['y'=4,'core'=2,'z'=8,'x'=4] {'x'}, dimensions={0} | all-to-all | bytes 2097152 | tf_op jit(solution)/shard_map/all_to_all | solution.py:18
  22.2 8.5 %all-to-all-start.1 = ((f32[8,32,256]{2,1,0:T(8,128)}), f32[8,32,256]{2,1,0:T(8,128)S(1)}, u32[]{:S(2)}, u32[]{:S(2)}) async-start(f32[8,32,256]{2,1,0:T(8,128)} %bitcast.2), calls=%async_computation.1 | async-start | bytes 524288 | tf_op jit(solution)/shard_map/all_to_all | solution.py:18
  30.7 4.0 %constant_dynamic-slice_fusion.5 = (f32[512,512]{1,0:T(8,128)}, f32[512,512]{1,0:T(8,128)}, f32[512,512]{1,0:T(8,128)S(1)}, f32[512,512]{1,0:T(8,128)}) fusion(f32[512,2048]{1,0:T(8,128)} %param.10, s32[]{:T(128)S(6)} %select_n.31, s32[]{:T(128)S(6)} %select_n.30, s32[]{:T(128)S(6)} %select_n.26, s32[]{:T(128)S(6)} %select_n.32), kind=kLoop, calls=%fused_computation.50 | loop fusion | bytes 8388624 | tf_op jit(solution)/shard_map/dynamic_slice | solution.py:41
  34.7 2.1 collective-permute-start.3
  36.7 4.7 %all-to-all-done.1 = f32[8,32,256]{2,1,0:T(8,128)S(1)} async-done(((f32[8,32,256]{2,1,0:T(8,128)}), f32[8,32,256]{2,1,0:T(8,128)S(1)}, u32[]{:S(2)}, u32[]{:S(2)}) %all-to-all-start.1) | async-done | bytes 262176 | tf_op jit(solution)/shard_map/all_to_all | solution.py:18
  42.0 11.5 %all_to_all.31 = f32[8,2,2048]{2,1,0:T(2,128)S(1)} all-to-all(f32[8,2,2048]{2,1,0:T(2,128)S(1)} %bitcast.51), channel_id=1, replica_groups=mesh['y'=4,'core'=2,'z'=8,'x'=4] {'z'}, dimensions={0} | all-to-all | bytes 262144 | tf_op jit(solution)/shard_map/all_to_all | solution.py:59
  54.4 5.5 %all-to-all-start.3 = ((f32[4,16,2048]{2,1,0:T(8,128)}), f32[4,16,2048]{2,1,0:T(8,128)S(1)}, u32[]{:S(2)}, u32[]{:S(2)}) async-start(f32[4,16,2048]{2,1,0:T(8,128)} %broadcast_in_dim.14), calls=%async_computation.3 | async-start | bytes 1048576 | tf_op jit(solution)/shard_map/all_to_all | solution.py:24
  61.5 24.7 %all-to-all-done.3 = f32[4,16,2048]{2,1,0:T(8,128)S(1)} async-done(((f32[4,16,2048]{2,1,0:T(8,128)}), f32[4,16,2048]{2,1,0:T(8,128)S(1)}, u32[]{:S(2)}, u32[]{:S(2)}) %all-to-all-start.3) | async-done | bytes 524320 | tf_op jit(solution)/shard_map/all_to_all | solution.py:24
  86.3 3.1 %collective-permute-start = (f32[64,2048]{1,0:T(8,128)S(1)}, f32[64,2048]{1,0:T(8,128)S(1)}, u32[]{:S(2)}, u32[]{:S(2)}) collective-permute-start(f32[64,2048]{1,0:T(8,128)S(1)} %pad_maximum_fusion.3), channel_id=1, source_target_pairs={{0,192},{64,0},{128,64},{192,128},{1,193},{65,1},{129,65},{193,129... | collective-permute-start | bytes 1572872 | tf_op jit(solution)/shard_map/ppermute | solution.py:14
  91.3 17.4 %collective-permute-done.4 = f32[512,512]{1,0:T(8,128)} collective-permute-done((f32[512,512]{1,0:T(8,128)}, f32[512,512]{1,0:T(8,128)}, u32[]{:S(2)}, u32[]{:S(2)}) %collective-permute-start.4) | collective-permute-done | bytes 1048608 | tf_op jit(solution)/shard_map/ppermute | solution.py:14
  109.7 1.8 fusion.11
  111.6 1.8 fusion.5
  113.4 1.8 fusion.8
  118.5 31.8 %all_to_all.32 = f32[8,32,1024]{2,1,0:T(8,128)S(1)} all-to-all(f32[8,32,1024]{2,1,0:T(8,128)S(1)} %bitcast.47), channel_id=1, replica_groups=mesh['y'=4,'core'=2,'z'=8,'x'=4] {'z'}, dimensions={0} | all-to-all | bytes 2097152 | tf_op jit(solution)/shard_map/all_to_all | solution.py:18
  151.6 3.6 %all-to-all-start.5 = ((f32[8,32,1024]{2,1,0:T(8,128)}), f32[8,32,1024]{2,1,0:T(8,128)S(1)}, u32[]{:S(2)}, u32[]{:S(2)}) async-start(f32[8,32,1024]{2,1,0:T(8,128)} %broadcast_in_dim.15), calls=%async_computation.5 | async-start | bytes 2097152 | tf_op jit(solution)/shard_map/all_to_all | solution.py:24
  155.1 1.7 constant_dynamic-slice_fusion.2
  156.9 2.2 %collective-permute-start.14 = (f32[256,512]{1,0:T(8,128)S(1)}, f32[256,512]{1,0:T(8,128)}, u32[]{:S(2)}, u32[]{:S(2)}) collective-permute-start(f32[256,512]{1,0:T(8,128)S(1)} %get-tuple-element.12), channel_id=1, source_target_pairs={{0,2},{1,3},{2,0},{3,1},{4,6},{5,7},{6,4},{7,5},{8,10},{9,11},{10,... | collective-permute-start | bytes 1572872 | tf_op jit(solution)/shard_map/ppermute | solution.py:14
  160.5 11.4 %collective-permute-done.11 = f32[256,512]{1,0:T(8,128)} collective-permute-done((f32[256,512]{1,0:T(8,128)S(1)}, f32[256,512]{1,0:T(8,128)}, u32[]{:S(2)}, u32[]{:S(2)}) %collective-permute-start.11) | collective-permute-done | bytes 524320 | tf_op jit(solution)/shard_map/ppermute | solution.py:14
  173.5 9.1 %collective-permute-done.17 = f32[256,512]{1,0:T(8,128)} collective-permute-done((f32[256,512]{1,0:T(8,128)S(1)}, f32[256,512]{1,0:T(8,128)}, u32[]{:S(2)}, u32[]{:S(2)}) %collective-permute-start.17) | collective-permute-done | bytes 524320 | tf_op jit(solution)/shard_map/ppermute | solution.py:14
  190.3 2.4 %collective-permute-start.16 = (f32[256,256]{1,0:T(8,128)S(1)}, f32[256,256]{1,0:T(8,128)S(1)}, u32[]{:S(2)}, u32[]{:S(2)}) collective-permute-start(f32[256,256]{1,0:T(8,128)S(1)} %convolution_add_fusion.4), channel_id=1, source_target_pairs={{0,2},{1,3},{2,0},{3,1},{4,6},{5,7},{6,4},{7,5},{8,10},{9,11},{10,... | collective-permute-start | bytes 786440 | tf_op jit(solution)/shard_map/ppermute | solution.py:14
  195.6 2.7 %collective-permute-start.19 = (f32[256,256]{1,0:T(8,128)S(1)}, f32[256,256]{1,0:T(8,128)S(1)}, u32[]{:S(2)}, u32[]{:S(2)}) collective-permute-start(f32[256,256]{1,0:T(8,128)S(1)} %convolution_add_fusion.3), channel_id=1, source_target_pairs={{0,1},{1,2},{2,3},{3,0},{4,5},{5,6},{6,7},{7,4},{8,9},{9,10},{10,1... | collective-permute-start | bytes 786440 | tf_op jit(solution)/shard_map/ppermute | solution.py:14
  201.5 3.4 %collective-permute-done.19 = f32[256,256]{1,0:T(8,128)S(1)} collective-permute-done((f32[256,256]{1,0:T(8,128)S(1)}, f32[256,256]{1,0:T(8,128)S(1)}, u32[]{:S(2)}, u32[]{:S(2)}) %collective-permute-start.19) | collective-permute-done | bytes 262176 | tf_op jit(solution)/shard_map/ppermute | solution.py:14
  205.1 2.8 %collective-permute-start.20 = (f32[64,256]{1,0:T(8,128)S(1)}, f32[64,256]{1,0:T(8,128)S(1)}, u32[]{:S(2)}, u32[]{:S(2)}) collective-permute-start(f32[64,256]{1,0:T(8,128)S(1)} %get-tuple-element.17), channel_id=1, source_target_pairs={{0,64},{64,128},{128,192},{192,0},{1,65},{65,129},{129,193},{193,1... | collective-permute-start | bytes 196616 | tf_op jit(solution)/shard_map/ppermute | solution.py:14
  207.9 2.9 %collective-permute-start.21 = (f32[64,256]{1,0:T(8,128)S(1)}, f32[64,256]{1,0:T(8,128)S(1)}, u32[]{:S(2)}, u32[]{:S(2)}) collective-permute-start(f32[64,256]{1,0:T(8,128)S(1)} %get-tuple-element.19), channel_id=1, source_target_pairs={{0,128},{64,192},{128,0},{192,64},{1,129},{65,193},{129,1},{193,65... | collective-permute-start | bytes 196616 | tf_op jit(solution)/shard_map/ppermute | solution.py:14
  (77 shorter events, 36.9 us)
Async XLA Ops:
  22.2 19.2 %all-to-all-start.1 = ((f32[8,32,256]{2,1,0:T(8,128)}), f32[8,32,256]{2,1,0:T(8,128)S(1)}, u32[]{:S(2)}, u32[]{:S(2)}) async-start(f32[8,32,256]{2,1,0:T(8,128)} %bitcast.2), calls=%async_computation.1 | async-start | bytes 524288 | tf_op jit(solution)/shard_map/all_to_all | solution.py:18
  34.7 55.3 %collective-permute-start.3 = (f32[512,512]{1,0:T(8,128)}, f32[512,512]{1,0:T(8,128)}, u32[]{:S(2)}, u32[]{:S(2)}) collective-permute-start(f32[512,512]{1,0:T(8,128)} %get-tuple-element.6), channel_id=1, source_target_pairs={{0,1},{1,2},{2,3},{3,0},{4,5},{5,6},{6,7},{7,4},{8,9},{9,10},{10,1... | collective-permute-start | bytes 3145736 | tf_op jit(solution)/shard_map/ppermute | solution.py:14
  54.4 31.7 %all-to-all-start.3 = ((f32[4,16,2048]{2,1,0:T(8,128)}), f32[4,16,2048]{2,1,0:T(8,128)S(1)}, u32[]{:S(2)}, u32[]{:S(2)}) async-start(f32[4,16,2048]{2,1,0:T(8,128)} %broadcast_in_dim.14), calls=%async_computation.3 | async-start | bytes 1048576 | tf_op jit(solution)/shard_map/all_to_all | solution.py:24
  59.9 31.4 %collective-permute-start.5 = (f32[512,512]{1,0:T(8,128)}, f32[512,512]{1,0:T(8,128)}, u32[]{:S(2)}, u32[]{:S(2)}) collective-permute-start(f32[512,512]{1,0:T(8,128)} %get-tuple-element.8), channel_id=1, source_target_pairs={{0,3},{1,0},{2,1},{3,2},{4,7},{5,4},{6,5},{7,6},{8,11},{9,8},{10,9... | collective-permute-start | bytes 3145736 | tf_op jit(solution)/shard_map/ppermute | solution.py:14
  60.8 47.9 %collective-permute-start.4 = (f32[512,512]{1,0:T(8,128)}, f32[512,512]{1,0:T(8,128)}, u32[]{:S(2)}, u32[]{:S(2)}) collective-permute-start(f32[512,512]{1,0:T(8,128)} %get-tuple-element.5), channel_id=1, source_target_pairs={{0,2},{1,3},{2,0},{3,1},{4,6},{5,7},{6,4},{7,5},{8,10},{9,11},{10,... | collective-permute-start | bytes 3145736 | tf_op jit(solution)/shard_map/ppermute | solution.py:14
  86.3 22.5 %collective-permute-start = (f32[64,2048]{1,0:T(8,128)S(1)}, f32[64,2048]{1,0:T(8,128)S(1)}, u32[]{:S(2)}, u32[]{:S(2)}) collective-permute-start(f32[64,2048]{1,0:T(8,128)S(1)} %pad_maximum_fusion.3), channel_id=1, source_target_pairs={{0,192},{64,0},{128,64},{192,128},{1,193},{65,1},{129,65},{193,129... | collective-permute-start | bytes 1572872 | tf_op jit(solution)/shard_map/ppermute | solution.py:14
  89.3 19.9 %collective-permute-start.1 = (f32[64,2048]{1,0:T(8,128)S(1)}, f32[64,2048]{1,0:T(8,128)S(1)}, u32[]{:S(2)}, u32[]{:S(2)}) collective-permute-start(f32[64,2048]{1,0:T(8,128)S(1)} %pad_maximum_fusion.3), channel_id=1, source_target_pairs={{0,128},{64,192},{128,0},{192,64},{1,129},{65,193},{129,1},{193,65... | collective-permute-start | bytes 1572872 | tf_op jit(solution)/shard_map/ppermute | solution.py:14
  90.0 19.5 %collective-permute-start.2 = (f32[64,2048]{1,0:T(8,128)S(1)}, f32[64,2048]{1,0:T(8,128)S(1)}, u32[]{:S(2)}, u32[]{:S(2)}) collective-permute-start(f32[64,2048]{1,0:T(8,128)S(1)} %pad_maximum_fusion.3), channel_id=1, source_target_pairs={{0,64},{64,128},{128,192},{192,0},{1,65},{65,129},{129,193},{193,1... | collective-permute-start | bytes 1572872 | tf_op jit(solution)/shard_map/ppermute | solution.py:14
  91.3 24.0 %collective-permute-start.6 = (f32[512,512]{1,0:T(8,128)S(1)}, f32[512,512]{1,0:T(8,128)S(1)}, u32[]{:S(2)}, u32[]{:S(2)}) collective-permute-start(f32[512,512]{1,0:T(8,128)S(1)} %get-tuple-element.7), channel_id=1, source_target_pairs={{0,32},{32,0},{1,33},{33,1},{2,34},{34,2},{3,35},{35,3},{4,36},{36... | collective-permute-start | bytes 3145736 | tf_op jit(solution)/shard_map/ppermute | solution.py:44
  108.7 7.8 %collective-permute-start.7 = (f32[512,512]{1,0:T(8,128)}, f32[512,512]{1,0:T(8,128)S(1)}, u32[]{:S(2)}, u32[]{:S(2)}) collective-permute-start(f32[512,512]{1,0:T(8,128)} %collective-permute-done.3), channel_id=1, source_target_pairs={{0,32},{32,0},{1,33},{33,1},{2,34},{34,2},{3,35},{35,3},{4,36},{36... | collective-permute-start | bytes 3145736 | tf_op jit(solution)/shard_map/ppermute | solution.py:44
  108.7 7.2 %collective-permute-start.9 = (f32[512,512]{1,0:T(8,128)}, f32[512,512]{1,0:T(8,128)S(1)}, u32[]{:S(2)}, u32[]{:S(2)}) collective-permute-start(f32[512,512]{1,0:T(8,128)} %collective-permute-done.5), channel_id=1, source_target_pairs={{0,32},{32,0},{1,33},{33,1},{2,34},{34,2},{3,35},{35,3},{4,36},{36... | collective-permute-start | bytes 3145736 | tf_op jit(solution)/shard_map/ppermute | solution.py:44
  109.2 8.6 %collective-permute-start.8 = (f32[512,512]{1,0:T(8,128)}, f32[512,512]{1,0:T(8,128)S(1)}, u32[]{:S(2)}, u32[]{:S(2)}) collective-permute-start(f32[512,512]{1,0:T(8,128)} %collective-permute-done.4), channel_id=1, source_target_pairs={{0,32},{32,0},{1,33},{33,1},{2,34},{34,2},{3,35},{35,3},{4,36},{36... | collective-permute-start | bytes 3145736 | tf_op jit(solution)/shard_map/ppermute | solution.py:44
  151.6 31.3 %all-to-all-start.5 = ((f32[8,32,1024]{2,1,0:T(8,128)}), f32[8,32,1024]{2,1,0:T(8,128)S(1)}, u32[]{:S(2)}, u32[]{:S(2)}) async-start(f32[8,32,1024]{2,1,0:T(8,128)} %broadcast_in_dim.15), calls=%async_computation.5 | async-start | bytes 2097152 | tf_op jit(solution)/shard_map/all_to_all | solution.py:24
  156.9 15.0 %collective-permute-start.11 = (f32[256,512]{1,0:T(8,128)S(1)}, f32[256,512]{1,0:T(8,128)}, u32[]{:S(2)}, u32[]{:S(2)}) collective-permute-start(f32[256,512]{1,0:T(8,128)S(1)} %get-tuple-element.9), channel_id=1, source_target_pairs={{0,1},{1,2},{2,3},{3,0},{4,5},{5,6},{6,7},{7,4},{8,9},{9,10},{10,1... | collective-permute-start | bytes 1572872 | tf_op jit(solution)/shard_map/ppermute | solution.py:14
  156.9 16.5 %collective-permute-start.14 = (f32[256,512]{1,0:T(8,128)S(1)}, f32[256,512]{1,0:T(8,128)}, u32[]{:S(2)}, u32[]{:S(2)}) collective-permute-start(f32[256,512]{1,0:T(8,128)S(1)} %get-tuple-element.12), channel_id=1, source_target_pairs={{0,2},{1,3},{2,0},{3,1},{4,6},{5,7},{6,4},{7,5},{8,10},{9,11},{10,... | collective-permute-start | bytes 1572872 | tf_op jit(solution)/shard_map/ppermute | solution.py:14
  159.2 23.5 %collective-permute-start.17 = (f32[256,512]{1,0:T(8,128)S(1)}, f32[256,512]{1,0:T(8,128)}, u32[]{:S(2)}, u32[]{:S(2)}) collective-permute-start(f32[256,512]{1,0:T(8,128)S(1)} %get-tuple-element.11), channel_id=1, source_target_pairs={{0,3},{1,0},{2,1},{3,2},{4,7},{5,4},{6,5},{7,6},{8,11},{9,8},{10,9... | collective-permute-start | bytes 1572872 | tf_op jit(solution)/shard_map/ppermute | solution.py:14
  171.8 12.5 %collective-permute-start.12 = (f32[256,512]{1,0:T(8,128)}, f32[256,512]{1,0:T(8,128)}, u32[]{:S(2)}, u32[]{:S(2)}) collective-permute-start(f32[256,512]{1,0:T(8,128)} %collective-permute-done.11), channel_id=1, source_target_pairs={{0,32},{32,0},{1,33},{33,1},{2,34},{34,2},{3,35},{35,3},{4,36},{36... | collective-permute-start | bytes 1572872 | tf_op jit(solution)/shard_map/ppermute | solution.py:44
  171.8 26.9 %collective-permute-start.10 = (f32[256,512]{1,0:T(8,128)S(1)}, f32[256,512]{1,0:T(8,128)}, u32[]{:S(2)}, u32[]{:S(2)}) collective-permute-start(f32[256,512]{1,0:T(8,128)S(1)} %get-tuple-element.10), channel_id=1, source_target_pairs={{0,32},{32,0},{1,33},{33,1},{2,34},{34,2},{3,35},{35,3},{4,36},{36... | collective-permute-start | bytes 1572872 | tf_op jit(solution)/shard_map/ppermute | solution.py:44
  173.5 15.4 %collective-permute-start.15 = (f32[256,512]{1,0:T(8,128)}, f32[256,512]{1,0:T(8,128)}, u32[]{:S(2)}, u32[]{:S(2)}) collective-permute-start(f32[256,512]{1,0:T(8,128)} %collective-permute-done.14), channel_id=1, source_target_pairs={{0,32},{32,0},{1,33},{33,1},{2,34},{34,2},{3,35},{35,3},{4,36},{36... | collective-permute-start | bytes 1572872 | tf_op jit(solution)/shard_map/ppermute | solution.py:44
  182.6 11.5 %collective-permute-start.18 = (f32[256,512]{1,0:T(8,128)}, f32[256,512]{1,0:T(8,128)}, u32[]{:S(2)}, u32[]{:S(2)}) collective-permute-start(f32[256,512]{1,0:T(8,128)} %collective-permute-done.17), channel_id=1, source_target_pairs={{0,32},{32,0},{1,33},{33,1},{2,34},{34,2},{3,35},{35,3},{4,36},{36... | collective-permute-start | bytes 1572872 | tf_op jit(solution)/shard_map/ppermute | solution.py:44
  185.8 14.4 %collective-permute-start.13 = (f32[256,256]{1,0:T(8,128)S(1)}, f32[256,256]{1,0:T(8,128)S(1)}, u32[]{:S(2)}, u32[]{:S(2)}) collective-permute-start(f32[256,256]{1,0:T(8,128)S(1)} %convolution_add_fusion.5), channel_id=1, source_target_pairs={{0,3},{1,0},{2,1},{3,2},{4,7},{5,4},{6,5},{7,6},{8,11},{9,8},{10,9... | collective-permute-start | bytes 786440 | tf_op jit(solution)/shard_map/ppermute | solution.py:14
  190.3 11.2 %collective-permute-start.16 = (f32[256,256]{1,0:T(8,128)S(1)}, f32[256,256]{1,0:T(8,128)S(1)}, u32[]{:S(2)}, u32[]{:S(2)}) collective-permute-start(f32[256,256]{1,0:T(8,128)S(1)} %convolution_add_fusion.4), channel_id=1, source_target_pairs={{0,2},{1,3},{2,0},{3,1},{4,6},{5,7},{6,4},{7,5},{8,10},{9,11},{10,... | collective-permute-start | bytes 786440 | tf_op jit(solution)/shard_map/ppermute | solution.py:14
  195.6 9.4 %collective-permute-start.19 = (f32[256,256]{1,0:T(8,128)S(1)}, f32[256,256]{1,0:T(8,128)S(1)}, u32[]{:S(2)}, u32[]{:S(2)}) collective-permute-start(f32[256,256]{1,0:T(8,128)S(1)} %convolution_add_fusion.3), channel_id=1, source_target_pairs={{0,1},{1,2},{2,3},{3,0},{4,5},{5,6},{6,7},{7,4},{8,9},{9,10},{10,1... | collective-permute-start | bytes 786440 | tf_op jit(solution)/shard_map/ppermute | solution.py:14
  205.1 7.2 %collective-permute-start.20 = (f32[64,256]{1,0:T(8,128)S(1)}, f32[64,256]{1,0:T(8,128)S(1)}, u32[]{:S(2)}, u32[]{:S(2)}) collective-permute-start(f32[64,256]{1,0:T(8,128)S(1)} %get-tuple-element.17), channel_id=1, source_target_pairs={{0,64},{64,128},{128,192},{192,0},{1,65},{65,129},{129,193},{193,1... | collective-permute-start | bytes 196616 | tf_op jit(solution)/shard_map/ppermute | solution.py:14
  (5 other events, 18.0 us)
where the time goes:
time: 218 us; the launch traced here: 216 us
  waiting for transfers between devices  76.8 us (35%)
  blocking collectives  60.9 us (28%)
  starting transfers between devices  44.5 us (20%)
  matrix products  21.5 us (10%)
  local copies, waits for them, and re-layouts  10.4 us (5%)
    all_to_all x2, blocking collectives, summed_share(): lax.all_to_all(array.reshape(size, array.shape[0] // size, array.shape[1]...  49.4 us
    ppermute x15, waiting for transfers between devices, shifted(): lax.ppermute(array, axis, [(i, (i + steps) % size) for i in range(size)])  47.1 us
    ppermute x15, starting transfers between devices, shifted(): lax.ppermute(array, axis, [(i, (i + steps) % size) for i in range(size)])  25.7 us
    all_to_all x2, waiting for transfers between devices, everyones(): gathered = lax.all_to_all(copies, axis, 0, 0)  24.9 us
    all_to_all x1, blocking collectives, on_device(): mine = lax.all_to_all(local, 'z', 0, 0).reshape(few * nz, coords)  11.5 us
    dot_general x8, matrix products, on_device(): lax.dot_general(whole[:, side * width:(side + 1) * width], blocks[k], (((...  10.6 us
    all_to_all x2, starting transfers between devices, everyones(): gathered = lax.all_to_all(copies, axis, 0, 0)  9.07 us
    dot_general x8, matrix products, on_device(): jnp.dot(these[:, k * rows:(k + 1) * rows], blocks[k], precision=HIGH, pre...  8.61 us
  transfers between devices with their start and end apart: 26, of which 13 were waited for; matrix products, arithmetic and copies ran while one was open for 12% of the time, Pallas kernels for 0%

commit v1 on v0

v1 whole, which is shorter than its diff:
```python
import jax
import jax.numpy as jnp
from jax import lax
from jax.experimental import pallas as pl
from jax.experimental.pallas import tpu as pltpu
from jax.sharding import Mesh, PartitionSpec as P


FETCH_ORDER = (0, 1, 3, 2)
f32, bf16 = jnp.float32, jnp.bfloat16
ANY = pl.BlockSpec(memory_space=pl.ANY)
WHOLE = pl.BlockSpec(memory_space=pltpu.VMEM)
SWAP = [(0, 1), (1, 0)]


def shifted(array, axis, size, steps):
    if steps % size == 0:
        return array
    return lax.ppermute(array, axis, [(i, (i + steps) % size) for i in range(size)])


def summed_share(array, axis, size):
    pieces = lax.all_to_all(array.reshape(size, array.shape[0] // size, array.shape[1]), axis, 0, 0)
    return jnp.sum(pieces, axis=0)


def everyones(array, axis, size):
    copies = jnp.broadcast_to(array[None], (size,) + array.shape)
    gathered = lax.all_to_all(copies, axis, 0, 0)
    return gathered.reshape((size * array.shape[0],) + array.shape[1:])


def halves(values):
    high = values.astype(bf16)
    return high, (values - high.astype(f32)).astype(bf16)


def product(left, right, dims):
    def dot(a, b):
        return lax.dot_general(a, b, (dims, ((), ())), preferred_element_type=f32)

    return dot(left[0], right[1]) + dot(left[1], right[0]) + dot(left[0], right[0])


def project(inputs, out_grads, proj_in, proj_out, steps):
    def kernel(inputs_ref, out_grads_ref, proj_in_ref, proj_out_ref, out_ref):
        pj = proj_in_ref.shape[1]
        out_ref[:, :pj] = jnp.dot(inputs_ref[...], proj_in_ref[...], preferred_element_type=f32)
        out_ref[:, pj:] = jnp.dot(out_grads_ref[...], proj_out_ref[...], preferred_element_type=f32)

    rows = inputs.shape[0] // steps
    columns = proj_in.shape[1] + proj_out.shape[1]

    def split(array):
        return pl.BlockSpec((rows, array.shape[1]), lambda i: (i, 0))

    def all_of(array):
        return pl.BlockSpec(array.shape, lambda i: (0, 0))

    return pl.pallas_call(
        kernel,
        grid=(steps,),
        in_specs=[split(inputs), split(out_grads), all_of(proj_in), all_of(proj_out)],
        out_specs=pl.BlockSpec((rows, columns), lambda i: (i, 0)),
        out_shape=jax.ShapeDtypeStruct((inputs.shape[0], columns), f32),
        name="project",
    )(inputs, out_grads, proj_in, proj_out)


def fetch(blocks, buffers, sems, i):
    return pltpu.make_async_copy(blocks[i], buffers.at[i], sems.at[i])


def precondition(owned, fisher, order):
    count, nx = len(owned), len(fisher[0])
    examples = owned[0].shape[0]
    rows, columns = fisher[0][0].shape

    def kernel(*refs):
        grads, blocks = refs[:count], refs[count : count + 2 * nx]
        out_ref, buffers, sems = refs[count + 2 * nx :]
        x = lax.axis_index("x")
        copies = [[fetch(blocks, buffers, sems, side * nx + k) for side in range(2)] for k in range(nx)]
        for k in order:
            for copy in copies[k]:
                copy.start()
        for at, k in enumerate(order):
            first = pl.multiple_of(((x - k) & (nx - 1)) * rows, rows)
            left = halves(jnp.concatenate([g[:, pl.ds(first, rows)] for g in grads], axis=0))
            for side in range(2):
                copies[k][side].wait()
                term = product(left, halves(buffers[side * nx + k]), ((1,), (0,)))
                where = slice(side * columns, (side + 1) * columns)
                if at:
                    out_ref[:, where] += term
                else:
                    out_ref[:, where] = term

    return pl.pallas_call(
        kernel,
        in_specs=[WHOLE] * count + [ANY] * (2 * nx),
        out_specs=WHOLE,
        out_shape=jax.ShapeDtypeStruct((count * examples, 2 * columns), f32),
        scratch_shapes=[pltpu.VMEM((2 * nx, rows, columns), f32), pltpu.SemaphoreType.DMA((2 * nx,))],
        name="precondition",
    )(*owned, *fisher[0], *fisher[1])


def score(whole, stored, ny):
    nx = len(stored[0])
    many, columns = stored[0][0].shape
    examples = whole.shape[0] // ny

    def kernel(*refs):
        whole_ref, blocks = refs[0], refs[1 : 1 + 2 * nx]
        out_ref, buffers, sems = refs[1 + 2 * nx :]
        x, y = lax.axis_index("x"), lax.axis_index("y")
        copies = [[fetch(blocks, buffers, sems, side * nx + k) for side in range(2)] for k in range(nx)]
        for pair in copies:
            for copy in pair:
                copy.start()
        left = [halves(whole_ref[:, side * columns : (side + 1) * columns]) for side in range(2)]
        for k in range(nx):
            for copy in copies[k]:
                copy.wait()
            total = None
            for side in range(2):
                term = product(left[side], halves(buffers[side * nx + k]), ((1,), (1,)))
                total = term if total is None else total + term
            for d in range(ny):
                place = ((y + d) & (ny - 1)) * nx + ((x - k) & (nx - 1))
                out_ref[place] = total[d * examples : (d + 1) * examples]

    return pl.pallas_call(
        kernel,
        in_specs=[WHOLE] + [ANY] * (2 * nx),
        out_specs=WHOLE,
        out_shape=jax.ShapeDtypeStruct((ny * nx, examples, many), f32),
        scratch_shapes=[pltpu.VMEM((2 * nx, many, columns), f32), pltpu.SemaphoreType.DMA((2 * nx,))],
        name="score",
    )(whole, *stored[0], *stored[1])


def on_device(sizes, inputs, out_grads, proj_in, proj_out, inv_fisher, store_grads):
    ny, nz, nx = sizes["y"], sizes["z"], sizes["x"]
    examples, tokens = inputs.shape[0], inputs.shape[1]
    pj, pk = proj_in.shape[1], proj_out.shape[1]
    x = lax.axis_index("x")

    width = inv_fisher.shape[1] // nx

    def spread(array):
        own, other = [], []
        for k in range(nx):
            piece = lax.dynamic_slice_in_dim(array, ((x + k) & (nx - 1)) * width, width, 1)
            piece = shifted(piece, "x", nx, k)
            own.append(piece)
            other.append(lax.ppermute(piece, "core", SWAP))
        return own, other

    fisher = spread(inv_fisher)
    stored = spread(store_grads)

    both = project(
        inputs.reshape(examples * tokens, -1), out_grads.reshape(examples * tokens, -1), proj_in, proj_out, nx
    )
    both = summed_share(both, "x", nx)
    both = summed_share(both, "z", nz)
    few = examples // (nx * nz)
    act = both[:, :pj].reshape(few, tokens, pj)
    grad = both[:, pj:].reshape(few, tokens, pk)
    local = jnp.einsum("etk,etj->ekj", grad, act, precision=lax.Precision.HIGHEST)
    local = local.reshape(few, nz, -1).transpose(1, 0, 2)
    coords = local.shape[2]
    mine = lax.all_to_all(local, "z", 0, 0).reshape(few * nz, coords)
    mine = everyones(mine, "x", nx)
    owned = []
    for d in range(ny):
        owned.append(shifted(mine, "y", ny, -d))
    part = precondition(owned, fisher, FETCH_ORDER)
    whole = everyones(summed_share(part, "z", nz), "z", nz)
    scores = score(whole, stored, ny)
    scores = lax.all_to_all(scores, ("y", "x"), 0, 0, tiled=True)
    return jnp.sum(scores, axis=0)


def solution(mesh):
    sizes = {"y": 4, "core": 2, "z": 8, "x": 4}
    named = Mesh(mesh.devices.reshape(tuple(sizes.values())), tuple(sizes))
    tensor, store = ("y", "core"), ("z", "x")
    placed = (
        P(tensor, None, store),
        P(tensor, None, store),
        P(store, None),
        P(store, None),
        P(store, tensor),
        P(store, tensor),
    )

    def run(*args):
        return on_device(sizes, *args)

    return jax.shard_map(run, mesh=named, in_specs=placed, out_specs=P(tensor, store), check_vma=False)
```

time: 218 us -> 233 us (1.069)
  blocking collectives: 60.9 us -> 82.7 us
  matrix products: 21.5 us -> 0.39 us
  Pallas kernels: 0 us -> 19.9 us
  starting transfers between devices: 44.5 us -> 36.3 us
    all_to_all x1 -> x2, blocking collectives: 11.5 us -> 50 us  [the longest x1 29.7 us: everyones(): gathered = lax.all_to_all(copies, axis, 0, 0)]
    all_to_all x2 -> x1, waiting for transfers between devices: 24.9 us -> 0.01 us  [everyones(): gathered = lax.all_to_all(copies, axis, 0, 0)]
    ppermute x15 -> x9, waiting for transfers between devices: 47.1 us -> 71.3 us  [shifted(): lax.ppermute(array, axis, [(i, (i + steps) % size) for i in range(size)])]
    dot_general x18 -> x0, matrix products: 21.2 us -> none  [the longest x8 10.6 us: on_device(): lax.dot_general(whole[:, side * width:(side + 1) * width], blocks[k], (((...]
    pallas_call x0 -> x3, Pallas kernels: none -> 19.9 us  [the longest x1 8.16 us: precondition(): pl.pallas_call(kernel, in_specs=[WHOLE] * count + [ANY] * (2 * nx), out_s...]
    all_to_all x2 -> x1, blocking collectives: 49.4 us -> 32.7 us  [summed_share(): lax.all_to_all(array.reshape(size, array.shape[0] // size, array.shape[1]...]
    ppermute x15 -> x9, starting transfers between devices: 25.7 us -> 11.1 us  [shifted(): lax.ppermute(array, axis, [(i, (i + steps) % size) for i in range(size)])]
    all_to_all x0 -> x1, starting transfers between devices: none -> 7.56 us  [on_device(): mine = lax.all_to_all(local, 'z', 0, 0).reshape(few * nz, coords)]
  transfers between devices with their start and end apart: 26 -> 21, of which waited for: 13 -> 8; matrix products, arithmetic and copies ran while one was open for 12% -> 3% of each run, Pallas kernels for 0% -> 0%
where the time goes in v1:
time: 233 us; the launch traced here: 230 us
  blocking collectives  82.7 us (35%)
  waiting for transfers between devices  79.1 us (34%)
  starting transfers between devices  36.3 us (16%)
  Pallas kernels  19.9 us (9%)
  local copies, waits for them, and re-layouts  9.78 us (4%)
    ppermute x9, waiting for transfers between devices, shifted(): lax.ppermute(array, axis, [(i, (i + steps) % size) for i in range(size)])  71.3 us
    all_to_all x1, blocking collectives, summed_share(): lax.all_to_all(array.reshape(size, array.shape[0] // size, array.shape[1]...  32.7 us
    all_to_all x1, blocking collectives, everyones(): gathered = lax.all_to_all(copies, axis, 0, 0)  29.7 us
    all_to_all x1, blocking collectives, on_device(): scores = lax.all_to_all(scores, ('y', 'x'), 0, 0, tiled=True)  20.3 us
    all_to_all x2, starting transfers between devices, summed_share(): lax.all_to_all(array.reshape(size, array.shape[0] // size, array.shape[1]...  13.2 us
    ppermute x9, starting transfers between devices, shifted(): lax.ppermute(array, axis, [(i, (i + steps) % size) for i in range(size)])  11.1 us
    pallas_call x1, Pallas kernels, precondition(): pl.pallas_call(kernel, in_specs=[WHOLE] * count + [ANY] * (2 * nx), out_s...  8.16 us
    all_to_all x1, starting transfers between devices, on_device(): mine = lax.all_to_all(local, 'z', 0, 0).reshape(few * nz, coords)  7.56 us
  transfers between devices with their start and end apart: 21, of which 8 were waited for; matrix products, arithmetic and copies ran while one was open for 3% of the time, Pallas kernels for 0%

profile of v1, /device:TPU:6, one launch (start us, length us, event | category | flops | bytes accessed | tf_op | source)
XLA Modules:
  0.0 229.9 jit_solution(7216961038422729186)
XLA Ops:
  0.0 4.3 %project.1 = f32[1024,256]{1,0:T(8,128)} custom-call(bf16[1024,896]{1,0:T(8,128)(2,1)} %bitcast.21, bf16[1024,256]{1,0:T(8,128)(2,1)} %bitcast.22, bf16[896,128]{1,0:T(8,128)(2,1)} %proj_in_ref.1, bf16[256,128]{1,0:T(8,128)(2,1)} %proj_out_ref.1), custom_call_target="tpu_custom_call" | custom-call | tf_op jit(solution)/shard_map/project/pallas_call | solution.py:60
  4.3 5.7 %all-to-all-start = ((f32[4,256,256]{2,1,0:T(8,128)}), f32[4,256,256]{2,1,0:T(8,128)S(1)}, u32[]{:S(2)}, u32[]{:S(2)}) async-start(f32[4,256,256]{2,1,0:T(8,128)} %bitcast.14), calls=%async_computation | async-start | bytes 2097152 | tf_op jit(solution)/shard_map/all_to_all | solution.py:23
  10.0 4.2 %constant_dynamic-slice_fusion.4 = (f32[512,512]{1,0:T(8,128)S(1)}, f32[512,512]{1,0:T(8,128)}, f32[512,512]{1,0:T(8,128)S(1)}, f32[512,512]{1,0:T(8,128)}) fusion(f32[512,2048]{1,0:T(8,128)} %param.10, s32[]{:T(128)S(6)} %select_n.19, s32[]{:T(128)S(6)} %select_n.17, s32[]{:T(128)S(6)} %select_n.16, s32[]{:T(128)S(6)} %select_n.18), kind=kLoop, calls=%fused_computation.5 | loop fusion | bytes 8388624 | tf_op jit(solution)/shard_map/dynamic_slice | solution.py:155
  14.2 2.9 %collective-permute-start.4 = (f32[512,512]{1,0:T(8,128)}, f32[512,512]{1,0:T(8,128)}, u32[]{:S(2)}, u32[]{:S(2)}) collective-permute-start(f32[512,512]{1,0:T(8,128)} %get-tuple-element.8), channel_id=1, source_target_pairs={{0,2},{1,3},{2,0},{3,1},{4,6},{5,7},{6,4},{7,5},{8,10},{9,11},{10,... | collective-permute-start | bytes 3145736 | tf_op jit(solution)/shard_map/ppermute | solution.py:19
  17.1 7.4 %all-to-all-done = f32[4,256,256]{2,1,0:T(8,128)S(1)} async-done(((f32[4,256,256]{2,1,0:T(8,128)}), f32[4,256,256]{2,1,0:T(8,128)S(1)}, u32[]{:S(2)}, u32[]{:S(2)}) %all-to-all-start) | async-done | bytes 1048608 | tf_op jit(solution)/shard_map/all_to_all | solution.py:23
  25.3 7.6 %all-to-all-start.1 = ((f32[8,32,256]{2,1,0:T(8,128)}), f32[8,32,256]{2,1,0:T(8,128)S(1)}, u32[]{:S(2)}, u32[]{:S(2)}) async-start(f32[8,32,256]{2,1,0:T(8,128)} %bitcast.3), calls=%async_computation.1 | async-start | bytes 524288 | tf_op jit(solution)/shard_map/all_to_all | solution.py:23
  32.8 13.6 %collective-permute-done.3.refs_5_ = f32[512,512]{1,0:T(8,128)} collective-permute-done((f32[512,512]{1,0:T(8,128)}, f32[512,512]{1,0:T(8,128)}, u32[]{:S(2)}, u32[]{:S(2)}) %collective-permute-start.3) | collective-permute-done | bytes 1048608 | tf_op jit(solution)/shard_map/ppermute | solution.py:19
  47.6 7.6 %all-to-all-start.2 = ((f32[8,2,2048]{2,1,0:T(2,128)}), f32[8,2,2048]{2,1,0:T(2,128)S(1)}, u32[]{:S(2)}, u32[]{:S(2)}) async-start(f32[8,2,2048]{2,1,0:T(2,128)} %bitcast.13), calls=%async_computation.2 | async-start | bytes 262144 | tf_op jit(solution)/shard_map/all_to_all | solution.py:175
  55.5 11.6 %collective-permute-done.5.refs_7_ = f32[512,512]{1,0:T(8,128)} collective-permute-done((f32[512,512]{1,0:T(8,128)S(1)}, f32[512,512]{1,0:T(8,128)}, u32[]{:S(2)}, u32[]{:S(2)}) %collective-permute-start.5) | collective-permute-done | bytes 1048608 | tf_op jit(solution)/shard_map/ppermute | solution.py:19
  67.2 29.7 %all_to_all.35 = f32[4,16,2048]{2,1,0:T(8,128)S(1)} all-to-all(f32[4,16,2048]{2,1,0:T(8,128)S(1)} %broadcast_in_dim.14), channel_id=1, replica_groups=mesh['y'=4,'core'=2,'z'=8,'x'=4] {'x'}, dimensions={0} | all-to-all | bytes 1048576 | tf_op jit(solution)/shard_map/all_to_all | solution.py:29
  96.9 3.0 %collective-permute-start = (f32[64,2048]{1,0:T(8,128)S(1)}, f32[64,2048]{1,0:T(8,128)S(1)}, u32[]{:S(2)}, u32[]{:S(2)}) collective-permute-start(f32[64,2048]{1,0:T(8,128)S(1)} %bitcast.17), channel_id=1, source_target_pairs={{0,192},{64,0},{128,64},{192,128},{1,193},{65,1},{129,65},{193,129... | collective-permute-start | bytes 1572872 | tf_op jit(solution)/shard_map/ppermute | solution.py:19
  100.6 1.0 collective-permute-start.2
  101.6 18.8 %collective-permute-done.refs_1_ = f32[64,2048]{1,0:T(8,128)S(1)} collective-permute-done((f32[64,2048]{1,0:T(8,128)S(1)}, f32[64,2048]{1,0:T(8,128)S(1)}, u32[]{:S(2)}, u32[]{:S(2)}) %collective-permute-start) | collective-permute-done | bytes 524320 | tf_op jit(solution)/shard_map/ppermute | solution.py:19
  120.4 3.7 %collective-permute-done.2.refs_3_ = f32[64,2048]{1,0:T(8,128)S(1)} collective-permute-done((f32[64,2048]{1,0:T(8,128)S(1)}, f32[64,2048]{1,0:T(8,128)S(1)}, u32[]{:S(2)}, u32[]{:S(2)}) %collective-permute-start.2) | collective-permute-done | bytes 524320 | tf_op jit(solution)/shard_map/ppermute | solution.py:19
  124.9 8.2 %precondition.1 = f32[256,1024]{1,0:T(8,128)} custom-call(f32[64,2048]{1,0:T(8,128)} %bitcast.20, f32[64,2048]{1,0:T(8,128)} %copy-done.11, f32[64,2048]{1,0:T(8,128)} %copy-done.12, f32[64,2048]{1,0:T(8,128)} %copy-done.14, f32[512,512]{1,0:T(8,128)} %copy-done.1, f32[512,512]{1,0:T(8,128)} %collective-permute-done.3.refs_5_, ...), custom_call_target="tpu_custom_call" | custom-call | tf_op jit(solution)/shard_map/precondition/pallas_call | solution.py:99
  133.0 32.7 %all_to_all.36 = f32[8,32,1024]{2,1,0:T(8,128)S(1)} all-to-all(f32[8,32,1024]{2,1,0:T(8,128)} %bitcast.16), channel_id=1, replica_groups=mesh['y'=4,'core'=2,'z'=8,'x'=4] {'z'}, dimensions={0} | all-to-all | bytes 2097152 | tf_op jit(solution)/shard_map/all_to_all | solution.py:23
  165.8 1.1 broadcast_in_dim.15
  166.9 3.6 %all-to-all-start.5 = ((f32[8,32,1024]{2,1,0:T(8,128)}), f32[8,32,1024]{2,1,0:T(8,128)S(1)}, u32[]{:S(2)}, u32[]{:S(2)}) async-start(f32[8,32,1024]{2,1,0:T(8,128)} %broadcast_in_dim.15), calls=%async_computation.5 | async-start | bytes 2097152 | tf_op jit(solution)/shard_map/all_to_all | solution.py:29
  170.7 2.2 collective-permute-start.10
  172.9 1.3 collective-permute-start.12
  174.2 20.7 %collective-permute-done.10.refs_2_ = f32[256,512]{1,0:T(8,128)S(1)} collective-permute-done((f32[256,512]{1,0:T(8,128)S(1)}, f32[256,512]{1,0:T(8,128)S(1)}, u32[]{:S(2)}, u32[]{:S(2)}) %collective-permute-start.10) | collective-permute-done | bytes 524320 | tf_op jit(solution)/shard_map/ppermute | solution.py:19
  195.5 3.0 %collective-permute-done.12.refs_4_ = f32[256,512]{1,0:T(8,128)S(1)} collective-permute-done((f32[256,512]{1,0:T(8,128)S(1)}, f32[256,512]{1,0:T(8,128)S(1)}, u32[]{:S(2)}, u32[]{:S(2)}) %collective-permute-start.12) | collective-permute-done | bytes 524320 | tf_op jit(solution)/shard_map/ppermute | solution.py:19
  201.5 7.4 %score.1 = f32[16,64,256]{2,1,0:T(8,128)} custom-call(f32[256,1024]{1,0:T(8,128)} %bitcast.15, f32[256,512]{1,0:T(8,128)} %copy-done.4, f32[256,512]{1,0:T(8,128)} %copy-done.6, f32[256,512]{1,0:T(8,128)} %copy-done.7, f32[256,512]{1,0:T(8,128)} %copy-done.8, f32[256,512]{1,0:T(8,128)} %copy-done.9, f32[256,512]{1,0:T(8,128)} %copy-done.10, ...), custom_call_target="tpu_custom_call" | custom-call | tf_op jit(solution)/shard_map/score/pallas_call | solution.py:134
  208.9 20.3 %all_to_all.37 = f32[16,64,256]{2,1,0:T(8,128)S(1)} all-to-all(f32[16,64,256]{2,1,0:T(8,128)} %score.1), channel_id=1, replica_groups=mesh['y'=4,'core'=2,'z'=8,'x'=4] {'y','x'}, dimensions={0} | all-to-all | bytes 2097152 | tf_op jit(solution)/shard_map/all_to_all | solution.py:183
  (67 shorter events, 8.4 us)
Async XLA Ops:
  4.3 20.2 %all-to-all-start = ((f32[4,256,256]{2,1,0:T(8,128)}), f32[4,256,256]{2,1,0:T(8,128)S(1)}, u32[]{:S(2)}, u32[]{:S(2)}) async-start(f32[4,256,256]{2,1,0:T(8,128)} %bitcast.14), calls=%async_computation | async-start | bytes 2097152 | tf_op jit(solution)/shard_map/all_to_all | solution.py:23
  14.1 82.8 %copy-start.1 = (f32[512,512]{1,0:T(8,128)}, f32[512,512]{1,0:T(8,128)S(1)}, u32[]{:S(2)}) copy-start(f32[512,512]{1,0:T(8,128)S(1)} %get-tuple-element.7.refs_4_) | copy-start | bytes 3145732
  14.1 32.3 %collective-permute-start.3 = (f32[512,512]{1,0:T(8,128)}, f32[512,512]{1,0:T(8,128)}, u32[]{:S(2)}, u32[]{:S(2)}) collective-permute-start(f32[512,512]{1,0:T(8,128)} %get-tuple-element.6), channel_id=1, source_target_pairs={{0,1},{1,2},{2,3},{3,0},{4,5},{5,6},{6,7},{7,4},{8,9},{9,10},{10,1... | collective-permute-start | bytes 3145736 | tf_op jit(solution)/shard_map/ppermute | solution.py:19
  14.2 41.0 %collective-permute-start.4 = (f32[512,512]{1,0:T(8,128)}, f32[512,512]{1,0:T(8,128)}, u32[]{:S(2)}, u32[]{:S(2)}) collective-permute-start(f32[512,512]{1,0:T(8,128)} %get-tuple-element.8), channel_id=1, source_target_pairs={{0,2},{1,3},{2,0},{3,1},{4,6},{5,7},{6,4},{7,5},{8,10},{9,11},{10,... | collective-permute-start | bytes 3145736 | tf_op jit(solution)/shard_map/ppermute | solution.py:19
  17.1 50.0 %collective-permute-start.5 = (f32[512,512]{1,0:T(8,128)S(1)}, f32[512,512]{1,0:T(8,128)}, u32[]{:S(2)}, u32[]{:S(2)}) collective-permute-start(f32[512,512]{1,0:T(8,128)S(1)} %get-tuple-element.5), channel_id=1, source_target_pairs={{0,3},{1,0},{2,1},{3,2},{4,7},{5,4},{6,5},{7,6},{8,11},{9,8},{10,9... | collective-permute-start | bytes 3145736 | tf_op jit(solution)/shard_map/ppermute | solution.py:19
  25.3 21.2 %all-to-all-start.1 = ((f32[8,32,256]{2,1,0:T(8,128)}), f32[8,32,256]{2,1,0:T(8,128)S(1)}, u32[]{:S(2)}, u32[]{:S(2)}) async-start(f32[8,32,256]{2,1,0:T(8,128)} %bitcast.3), calls=%async_computation.1 | async-start | bytes 524288 | tf_op jit(solution)/shard_map/all_to_all | solution.py:23
  32.8 67.1 %collective-permute-start.6 = (f32[512,512]{1,0:T(8,128)S(1)}, f32[512,512]{1,0:T(8,128)}, u32[]{:S(2)}, u32[]{:S(2)}) collective-permute-start(f32[512,512]{1,0:T(8,128)S(1)} %get-tuple-element.7.refs_4_), channel_id=1, source_target_pairs={{0,32},{32,0},{1,33},{33,1},{2,34},{34,2},{3,35},{35,3},{4,36},{36... | collective-permute-start | bytes 3145736 | tf_op jit(solution)/shard_map/ppermute | solution.py:158
  46.4 54.2 %collective-permute-start.7 = (f32[512,512]{1,0:T(8,128)}, f32[512,512]{1,0:T(8,128)}, u32[]{:S(2)}, u32[]{:S(2)}) collective-permute-start(f32[512,512]{1,0:T(8,128)} %collective-permute-done.3.refs_5_), channel_id=1, source_target_pairs={{0,32},{32,0},{1,33},{33,1},{2,34},{34,2},{3,35},{35,3},{4,36},{36... | collective-permute-start | bytes 3145736 | tf_op jit(solution)/shard_map/ppermute | solution.py:158
  47.6 19.5 %all-to-all-start.2 = ((f32[8,2,2048]{2,1,0:T(2,128)}), f32[8,2,2048]{2,1,0:T(2,128)S(1)}, u32[]{:S(2)}, u32[]{:S(2)}) async-start(f32[8,2,2048]{2,1,0:T(2,128)} %bitcast.13), calls=%async_computation.2 | async-start | bytes 262144 | tf_op jit(solution)/shard_map/all_to_all | solution.py:175
  55.2 46.4 %collective-permute-start.8 = (f32[512,512]{1,0:T(8,128)}, f32[512,512]{1,0:T(8,128)}, u32[]{:S(2)}, u32[]{:S(2)}) collective-permute-start(f32[512,512]{1,0:T(8,128)} %collective-permute-done.4.refs_6_), channel_id=1, source_target_pairs={{0,32},{32,0},{1,33},{33,1},{2,34},{34,2},{3,35},{35,3},{4,36},{36... | collective-permute-start | bytes 3145736 | tf_op jit(solution)/shard_map/ppermute | solution.py:158
  67.1 34.5 %collective-permute-start.9 = (f32[512,512]{1,0:T(8,128)}, f32[512,512]{1,0:T(8,128)S(1)}, u32[]{:S(2)}, u32[]{:S(2)}) collective-permute-start(f32[512,512]{1,0:T(8,128)} %collective-permute-done.5.refs_7_), channel_id=1, source_target_pairs={{0,32},{32,0},{1,33},{33,1},{2,34},{34,2},{3,35},{35,3},{4,36},{36... | collective-permute-start | bytes 3145736 | tf_op jit(solution)/shard_map/ppermute | solution.py:158
  96.9 27.1 %copy-start.2 = (f32[4,16,2048]{2,1,0:T(8,128)}, f32[4,16,2048]{2,1,0:T(8,128)S(1)}, u32[]{:S(2)}) copy-start(f32[4,16,2048]{2,1,0:T(8,128)S(1)} %all_to_all.35) | copy-start | bytes 1572868
  96.9 23.4 %collective-permute-start = (f32[64,2048]{1,0:T(8,128)S(1)}, f32[64,2048]{1,0:T(8,128)S(1)}, u32[]{:S(2)}, u32[]{:S(2)}) collective-permute-start(f32[64,2048]{1,0:T(8,128)S(1)} %bitcast.17), channel_id=1, source_target_pairs={{0,192},{64,0},{128,64},{192,128},{1,193},{65,1},{129,65},{193,129... | collective-permute-start | bytes 1572872 | tf_op jit(solution)/shard_map/ppermute | solution.py:19
  99.9 20.4 %collective-permute-start.1 = (f32[64,2048]{1,0:T(8,128)S(1)}, f32[64,2048]{1,0:T(8,128)S(1)}, u32[]{:S(2)}, u32[]{:S(2)}) collective-permute-start(f32[64,2048]{1,0:T(8,128)S(1)} %bitcast.18), channel_id=1, source_target_pairs={{0,128},{64,192},{128,0},{192,64},{1,129},{65,193},{129,1},{193,65... | collective-permute-start | bytes 1572872 | tf_op jit(solution)/shard_map/ppermute | solution.py:19
  100.6 23.5 %collective-permute-start.2 = (f32[64,2048]{1,0:T(8,128)S(1)}, f32[64,2048]{1,0:T(8,128)S(1)}, u32[]{:S(2)}, u32[]{:S(2)}) collective-permute-start(f32[64,2048]{1,0:T(8,128)S(1)} %bitcast.19), channel_id=1, source_target_pairs={{0,64},{64,128},{128,192},{192,0},{1,65},{65,129},{129,193},{193,1... | collective-permute-start | bytes 1572872 | tf_op jit(solution)/shard_map/ppermute | solution.py:19
  166.9 33.6 %all-to-all-start.5 = ((f32[8,32,1024]{2,1,0:T(8,128)}), f32[8,32,1024]{2,1,0:T(8,128)S(1)}, u32[]{:S(2)}, u32[]{:S(2)}) async-start(f32[8,32,1024]{2,1,0:T(8,128)} %broadcast_in_dim.15), calls=%async_computation.5 | async-start | bytes 2097152 | tf_op jit(solution)/shard_map/all_to_all | solution.py:29
  170.7 27.8 %copy-start.4 = (f32[256,512]{1,0:T(8,128)}, f32[256,512]{1,0:T(8,128)S(1)}, u32[]{:S(2)}) copy-start(f32[256,512]{1,0:T(8,128)S(1)} %get-tuple-element.11.refs_1_) | copy-start | bytes 1572868
  170.7 24.3 %collective-permute-start.10 = (f32[256,512]{1,0:T(8,128)S(1)}, f32[256,512]{1,0:T(8,128)S(1)}, u32[]{:S(2)}, u32[]{:S(2)}) collective-permute-start(f32[256,512]{1,0:T(8,128)S(1)} %get-tuple-element.10), channel_id=1, source_target_pairs={{0,1},{1,2},{2,3},{3,0},{4,5},{5,6},{6,7},{7,4},{8,9},{9,10},{10,1... | collective-permute-start | bytes 1572872 | tf_op jit(solution)/shard_map/ppermute | solution.py:19
  172.8 22.1 %collective-permute-start.11 = (f32[256,512]{1,0:T(8,128)S(1)}, f32[256,512]{1,0:T(8,128)S(1)}, u32[]{:S(2)}, u32[]{:S(2)}) collective-permute-start(f32[256,512]{1,0:T(8,128)S(1)} %get-tuple-element.12), channel_id=1, source_target_pairs={{0,2},{1,3},{2,0},{3,1},{4,6},{5,7},{6,4},{7,5},{8,10},{9,11},{10,... | collective-permute-start | bytes 1572872 | tf_op jit(solution)/shard_map/ppermute | solution.py:19
  172.9 25.5 %collective-permute-start.12 = (f32[256,512]{1,0:T(8,128)S(1)}, f32[256,512]{1,0:T(8,128)S(1)}, u32[]{:S(2)}, u32[]{:S(2)}) collective-permute-start(f32[256,512]{1,0:T(8,128)S(1)} %get-tuple-element.9), channel_id=1, source_target_pairs={{0,3},{1,0},{2,1},{3,2},{4,7},{5,4},{6,5},{7,6},{8,11},{9,8},{10,9... | collective-permute-start | bytes 1572872 | tf_op jit(solution)/shard_map/ppermute | solution.py:19
  174.2 24.2 %collective-permute-start.13 = (f32[256,512]{1,0:T(8,128)S(1)}, f32[256,512]{1,0:T(8,128)S(1)}, u32[]{:S(2)}, u32[]{:S(2)}) collective-permute-start(f32[256,512]{1,0:T(8,128)S(1)} %get-tuple-element.11.refs_1_), channel_id=1, source_target_pairs={{0,32},{32,0},{1,33},{33,1},{2,34},{34,2},{3,35},{35,3},{4,36},{36... | collective-permute-start | bytes 1572872 | tf_op jit(solution)/shard_map/ppermute | solution.py:158
  195.0 3.5 %collective-permute-start.14 = (f32[256,512]{1,0:T(8,128)S(1)}, f32[256,512]{1,0:T(8,128)S(1)}, u32[]{:S(2)}, u32[]{:S(2)}) collective-permute-start(f32[256,512]{1,0:T(8,128)S(1)} %collective-permute-done.10.refs_2_), channel_id=1, source_target_pairs={{0,32},{32,0},{1,33},{33,1},{2,34},{34,2},{3,35},{35,3},{4,36},{36... | collective-permute-start | bytes 1572872 | tf_op jit(solution)/shard_map/ppermute | solution.py:158
  195.0 3.5 %collective-permute-start.15 = (f32[256,512]{1,0:T(8,128)S(1)}, f32[256,512]{1,0:T(8,128)S(1)}, u32[]{:S(2)}, u32[]{:S(2)}) collective-permute-start(f32[256,512]{1,0:T(8,128)S(1)} %collective-permute-done.11.refs_3_), channel_id=1, source_target_pairs={{0,32},{32,0},{1,33},{33,1},{2,34},{34,2},{3,35},{35,3},{4,36},{36... | collective-permute-start | bytes 1572872 | tf_op jit(solution)/shard_map/ppermute | solution.py:158
  198.4 2.0 collective-permute-start.16
  (12 other events, 53.3 us)

commit v2 on v1

v2 whole, which is shorter than its diff:
```python
import jax
import jax.numpy as jnp
from jax import lax
from jax.experimental import pallas as pl
from jax.experimental.pallas import tpu as pltpu
from jax.sharding import Mesh, PartitionSpec as P


SWAP = [(0, 1), (1, 0)]


def shifted(array, axis, size, steps):
    if steps % size == 0:
        return array
    return lax.ppermute(array, axis, [(i, (i + steps) % size) for i in range(size)])


def pieces_of(array, axis):
    return lax.all_to_all(array, axis, 0, 0)


def summed_share(array, axis, size):
    pieces = pieces_of(array.reshape(size, array.shape[0] // size, array.shape[1]), axis)
    return summed(pieces)


def summed(pieces):
    return jnp.sum(pieces, axis=0)


f32, bf16 = jnp.float32, jnp.bfloat16
WHOLE = pl.BlockSpec(memory_space=pltpu.VMEM)
ROOM = pltpu.CompilerParams(vmem_limit_bytes=24 * 2**20)


def near(array):
    return pltpu.with_memory_space_constraint(array, pltpu.VMEM)


def halves(values):
    high = values.astype(bf16)
    return high, (values - high.astype(f32)).astype(bf16)


def product(left, right, dims):
    def dot(a, b):
        return lax.dot_general(a, b, (dims, ((), ())), preferred_element_type=f32)

    return dot(left[0], right[1]) + dot(left[1], right[0]) + dot(left[0], right[0])


def project(inputs, out_grads, proj_in, proj_out, steps):
    def kernel(inputs_ref, out_grads_ref, proj_in_ref, proj_out_ref, out_ref):
        pj = proj_in_ref.shape[1]
        out_ref[:, :pj] = jnp.dot(inputs_ref[...], proj_in_ref[...], preferred_element_type=f32)
        out_ref[:, pj:] = jnp.dot(out_grads_ref[...], proj_out_ref[...], preferred_element_type=f32)

    rows = inputs.shape[0] // steps
    columns = proj_in.shape[1] + proj_out.shape[1]

    def split(array):
        return pl.BlockSpec((rows, array.shape[1]), lambda i: (i, 0))

    def all_of(array):
        return pl.BlockSpec(array.shape, lambda i: (0, 0))

    return pl.pallas_call(
        kernel,
        grid=(steps,),
        in_specs=[split(inputs), split(out_grads), all_of(proj_in), all_of(proj_out)],
        out_specs=pl.BlockSpec((rows, columns), lambda i: (i, 0)),
        out_shape=jax.ShapeDtypeStruct((inputs.shape[0], columns), f32),
        name="project",
        compiler_params=ROOM,
    )(inputs, out_grads, proj_in, proj_out)


def store_rows(out_ref, count, where, values, add):
    nz, columns = out_ref.shape[0], values.shape[1]
    values = values.reshape(count, nz, -1, columns)
    each = values.shape[2]
    for d in range(count):
        rows = slice(d * each, (d + 1) * each)
        if add:
            out_ref[:, rows, where] += values[d]
        else:
            out_ref[:, rows, where] = values[d]


def precondition(owned, fisher, nz):
    count, nx = len(owned), len(fisher[0])
    examples = owned[0].shape[0]
    rows, columns = fisher[0][0].shape

    def kernel(*refs):
        grads, blocks, out_ref = refs[:count], refs[count : count + 2 * nx], refs[count + 2 * nx]
        x = lax.axis_index("x")
        for k in range(nx):
            first = pl.multiple_of(((x - k) & (nx - 1)) * rows, rows)
            left = halves(jnp.concatenate([g[:, pl.ds(first, rows)] for g in grads], axis=0))
            for side in range(2):
                term = product(left, halves(blocks[side * nx + k][...]), ((1,), (0,)))
                store_rows(out_ref, count, slice(side * columns, (side + 1) * columns), term, k > 0)

    return pl.pallas_call(
        kernel,
        in_specs=[WHOLE] * (count + 2 * nx),
        out_specs=WHOLE,
        out_shape=pltpu.VMEM((nz, count * examples // nz, 2 * columns), f32),
        compiler_params=ROOM,
    )(*[near(g) for g in owned], *[near(f) for f in fisher[0] + fisher[1]])


def sum_copies(first, second):
    few, columns = first.shape
    nz, many = second.shape[:2]

    def kernel(first_ref, second_ref, out_ref):
        total = jnp.concatenate([first_ref[...], jnp.sum(second_ref[...], axis=0)], axis=0)
        for z in range(nz):
            out_ref[z] = total

    return pl.pallas_call(
        kernel,
        in_specs=[WHOLE] * 2,
        out_specs=WHOLE,
        out_shape=pltpu.VMEM((nz, few + many, columns), f32),
        name="sum_copies",
        compiler_params=ROOM,
    )(near(first), near(second))


def score(whole, stored, ny):
    nx = len(stored[0])
    many, columns = stored[0][0].shape
    nz = whole.shape[0]
    examples = nz * whole.shape[1] // ny

    def kernel(*refs):
        whole_ref, blocks = refs[0], refs[1 : 1 + 2 * nx]
        out_ref = refs[1 + 2 * nx]
        x, y = lax.axis_index("x"), lax.axis_index("y")
        left = []
        for side in range(2):
            values = whole_ref[:, :, side * columns : (side + 1) * columns]
            left.append(halves(values.reshape(ny * examples, columns)))
        for k in range(nx):
            total = None
            for side in range(2):
                term = product(left[side], halves(blocks[side * nx + k][...]), ((1,), (1,)))
                total = term if total is None else total + term
            total = total.reshape(nz, ny, examples // nz, many)
            for d in range(ny):
                place = ((y + d) & (ny - 1)) * nx + ((x - k) & (nx - 1))
                out_ref[place] = total[:, d].reshape(examples, many)

    return pl.pallas_call(
        kernel,
        in_specs=[WHOLE] * (1 + 2 * nx),
        out_specs=WHOLE,
        out_shape=pltpu.VMEM((ny * nx, examples, many), f32),
        name="score",
        compiler_params=ROOM,
    )(near(whole), *[near(s) for s in stored[0] + stored[1]])


def on_device(sizes, inputs, out_grads, proj_in, proj_out, inv_fisher, store_grads):
    ny, nz, nx = sizes["y"], sizes["z"], sizes["x"]
    examples, tokens = inputs.shape[0], inputs.shape[1]
    pj, pk = proj_in.shape[1], proj_out.shape[1]
    x = lax.axis_index("x")

    width = inv_fisher.shape[1] // nx

    def spread(array):
        own, other = [], []
        for k in range(nx):
            piece = lax.dynamic_slice_in_dim(array, ((x + k) & (nx - 1)) * width, width, 1)
            piece = shifted(piece, "x", nx, k)
            own.append(piece)
            other.append(lax.ppermute(piece, "core", SWAP))
        return own, other

    fisher = spread(inv_fisher)
    stored = spread(store_grads)

    both = project(
        inputs.reshape(examples * tokens, -1), out_grads.reshape(examples * tokens, -1), proj_in, proj_out, nx
    )
    both = summed_share(both, "x", nx)
    both = summed_share(both, "z", nz)
    few = examples // (nx * nz)
    act = both[:, :pj].reshape(few, tokens, pj)
    grad = both[:, pj:].reshape(few, tokens, pk)
    local = jnp.einsum("etk,etj->ekj", grad, act, precision=lax.Precision.HIGHEST)
    local = local.reshape(few, nz, -1).transpose(1, 0, 2)
    coords = local.shape[2]
    mine = pieces_of(local, "z").reshape(few * nz, coords)
    mine = pieces_of(jnp.broadcast_to(mine[None], (nx,) + mine.shape), "x")
    mine = mine.reshape(nx * few * nz, coords)
    owned = []
    for d in range(ny):
        owned.append(shifted(mine, "y", ny, -d))
    ahead = precondition(owned[:1], fisher, nz)
    ahead = summed(pieces_of(ahead, "z"))
    rest = precondition(owned[1:], fisher, nz)
    rest = pieces_of(rest, "z")
    whole = pieces_of(sum_copies(ahead, rest), "z")
    scores = pieces_of(score(whole, stored, ny), ("y", "x"))
    return jnp.sum(scores, axis=0)


def solution(mesh):
    sizes = {"y": 4, "core": 2, "z": 8, "x": 4}
    named = Mesh(mesh.devices.reshape(tuple(sizes.values())), tuple(sizes))
    tensor, store = ("y", "core"), ("z", "x")
    placed = (
        P(tensor, None, store),
        P(tensor, None, store),
        P(store, None),
        P(store, None),
        P(store, tensor),
        P(store, tensor),
    )

    def run(*args):
        return on_device(sizes, *args)

    return jax.shard_map(run, mesh=named, in_specs=placed, out_specs=P(tensor, store), check_vma=False)
```

time: 233 us -> 228 us (0.979)
  blocking collectives: 82.7 us -> 49.4 us
  waiting for transfers between devices: 79.1 us -> 100 us
  local copies, waits for them, and re-layouts: 9.78 us -> 18.6 us
  Pallas kernels: 19.9 us -> 16.6 us
    all_to_all x3, blocking collectives: 82.7 us -> 49.4 us  [pieces_of(): return lax.all_to_all(array, axis, 0, 0)]
    all_to_all x4 -> x5, waiting for transfers between devices: 7.45 us -> 30.9 us  [pieces_of(): return lax.all_to_all(array, axis, 0, 0)]
    unnamed x30 -> x26, local copies, waits for them, and re-layouts: 3.41 us -> 12.6 us
    pallas_call x2 -> x4, Pallas kernels: 15.6 us -> 14.3 us  [the longest x2 11.4 us: precondition(): pl.pallas_call(kernel, in_specs=[WHOLE] * (count + 2 * nx), out_specs=WHO...]
    all_to_all x4 -> x5, starting transfers between devices: 24.4 us -> 24.8 us  [pieces_of(): return lax.all_to_all(array, axis, 0, 0)]
  transfers between devices with their start and end apart: 21 -> 22, of which waited for: 8 -> 9; matrix products, arithmetic and copies ran while one was open for 3% -> 4% of each run, Pallas kernels for 0% -> 5%
where the time goes in v2:
time: 228 us; the launch traced here: 225 us
  waiting for transfers between devices  100 us (44%)
  blocking collectives  49.4 us (22%)
  starting transfers between devices  36.4 us (16%)
  local copies, waits for them, and re-layouts  18.6 us (8%)
  Pallas kernels  16.6 us (7%)
  other arithmetic  2.76 us (1%)
    ppermute x9, waiting for transfers between devices, shifted(): lax.ppermute(array, axis, [(i, (i + steps) % size) for i in range(size)])  69.4 us
    all_to_all x3, blocking collectives, pieces_of(): return lax.all_to_all(array, axis, 0, 0)  49.4 us
    all_to_all x5, waiting for transfers between devices, pieces_of(): return lax.all_to_all(array, axis, 0, 0)  30.9 us
    all_to_all x5, starting transfers between devices, pieces_of(): return lax.all_to_all(array, axis, 0, 0)  24.8 us
    unnamed x26, local copies, waits for them, and re-layouts  12.6 us
    pallas_call x2, Pallas kernels, precondition(): pl.pallas_call(kernel, in_specs=[WHOLE] * (count + 2 * nx), out_specs=WHO...  11.4 us
    ppermute x9, starting transfers between devices, shifted(): lax.ppermute(array, axis, [(i, (i + steps) % size) for i in range(size)])  11.1 us
    dynamic_slice x2, local copies, waits for them, and re-layouts, spread(): piece = lax.dynamic_slice_in_dim(array, (x + k & nx - 1) * width, width, 1)  5.71 us
  transfers between devices with their start and end apart: 22, of which 9 were waited for; matrix products, arithmetic and copies ran while one was open for 4% of the time, Pallas kernels for 5%

profile of v2, /device:TPU:6, one launch (start us, length us, event | category | flops | bytes accessed | tf_op | source)
XLA Modules:
  0.0 224.6 jit_solution(381733487322442356)
XLA Ops:
  4.3 2.3 %project.1 = f32[1024,256]{1,0:T(8,128)} custom-call(bf16[1024,896]{1,0:T(8,128)(2,1)S(1)} %bitcast.12, bf16[1024,256]{1,0:T(8,128)(2,1)S(1)} %bitcast.13, bf16[896,128]{1,0:T(8,128)(2,1)S(1)} %copy-done.11, bf16[256,128]{1,0:T(8,128)(2,1)S(1)} %copy-done.12), custom_call_target="tpu_custom_call" | custom-call | tf_op jit(solution)/shard_map/project/pallas_call | solution.py:67
  6.7 6.4 %all-to-all-start = ((f32[4,256,256]{2,1,0:T(8,128)}), f32[4,256,256]{2,1,0:T(8,128)}, u32[]{:S(2)}, u32[]{:S(2)}) async-start(f32[4,256,256]{2,1,0:T(8,128)} %bitcast.2), calls=%async_computation | async-start | bytes 2097152 | tf_op jit(solution)/shard_map/all_to_all | solution.py:19
  13.0 4.0 %constant_dynamic-slice_fusion.4 = (f32[512,512]{1,0:T(8,128)}, f32[512,512]{1,0:T(8,128)}, f32[512,512]{1,0:T(8,128)S(1)}, f32[512,512]{1,0:T(8,128)}) fusion(f32[512,2048]{1,0:T(8,128)} %param.10, s32[]{:T(128)S(6)} %select_n.19, s32[]{:T(128)S(6)} %select_n.17, s32[]{:T(128)S(6)} %select_n.16, s32[]{:T(128)S(6)} %select_n.18), kind=kLoop, calls=%fused_computation.5 | loop fusion | bytes 8388624 | tf_op jit(solution)/shard_map/dynamic_slice | solution.py:178
  17.1 2.9 %collective-permute-start.1 = (f32[512,512]{1,0:T(8,128)}, f32[512,512]{1,0:T(8,128)S(1)}, u32[]{:S(2)}, u32[]{:S(2)}) collective-permute-start(f32[512,512]{1,0:T(8,128)} %get-tuple-element.8), channel_id=1, source_target_pairs={{0,2},{1,3},{2,0},{3,1},{4,6},{5,7},{6,4},{7,5},{8,10},{9,11},{10,... | collective-permute-start | bytes 3145736 | tf_op jit(solution)/shard_map/ppermute | solution.py:15
  20.0 7.6 %all-to-all-done = f32[4,256,256]{2,1,0:T(8,128)} async-done(((f32[4,256,256]{2,1,0:T(8,128)}), f32[4,256,256]{2,1,0:T(8,128)}, u32[]{:S(2)}, u32[]{:S(2)}) %all-to-all-start) | async-done | bytes 1048608 | tf_op jit(solution)/shard_map/all_to_all | solution.py:19
  27.6 2.0 reduce_sum.36
  29.6 6.9 %all-to-all-start.1 = ((f32[8,32,256]{2,1,0:T(8,128)}), f32[8,32,256]{2,1,0:T(8,128)S(1)}, u32[]{:S(2)}, u32[]{:S(2)}) async-start(f32[8,32,256]{2,1,0:T(8,128)} %bitcast.3), calls=%async_computation.1 | async-start | bytes 524288 | tf_op jit(solution)/shard_map/all_to_all | solution.py:19
  36.6 12.8 %collective-permute-done.refs_2_.refs_4_ = f32[512,512]{1,0:T(8,128)S(1)} collective-permute-done((f32[512,512]{1,0:T(8,128)}, f32[512,512]{1,0:T(8,128)S(1)}, u32[]{:S(2)}, u32[]{:S(2)}) %collective-permute-start) | collective-permute-done | bytes 1048608 | tf_op jit(solution)/shard_map/ppermute | solution.py:15
  50.0 19.2 %collective-permute-done.2.refs_4_.refs_6_ = f32[512,512]{1,0:T(8,128)} collective-permute-done((f32[512,512]{1,0:T(8,128)}, f32[512,512]{1,0:T(8,128)}, u32[]{:S(2)}, u32[]{:S(2)}) %collective-permute-start.2) | collective-permute-done | bytes 1048608 | tf_op jit(solution)/shard_map/ppermute | solution.py:15
  69.7 18.6 %all_to_all.40 = f32[8,2,2048]{2,1,0:T(2,128)S(1)} all-to-all(f32[8,2,2048]{2,1,0:T(2,128)S(1)} %bitcast.14), channel_id=1, replica_groups=mesh['y'=4,'core'=2,'z'=8,'x'=4] {'z'}, dimensions={0} | all-to-all | bytes 262144 | tf_op jit(solution)/shard_map/all_to_all | solution.py:19
  88.4 11.2 %all_to_all.41 = f32[4,16,2048]{2,1,0:T(8,128)} all-to-all(f32[4,16,2048]{2,1,0:T(8,128)S(1)} %broadcast_in_dim.8), channel_id=1, replica_groups=mesh['y'=4,'core'=2,'z'=8,'x'=4] {'x'}, dimensions={0} | all-to-all | bytes 1048576 | tf_op jit(solution)/shard_map/all_to_all | solution.py:19
  99.6 3.0 %collective-permute-start.7 = (f32[64,2048]{1,0:T(8,128)}, f32[64,2048]{1,0:T(8,128)}, u32[]{:S(2)}, u32[]{:S(2)}) collective-permute-start(f32[64,2048]{1,0:T(8,128)} %bitcast.7.refs_0_), channel_id=1, source_target_pairs={{0,192},{64,0},{128,64},{192,128},{1,193},{65,1},{129,65},{193,129... | collective-permute-start | bytes 1572872 | tf_op jit(solution)/shard_map/ppermute | solution.py:15
  104.2 5.7 %shard_map.64 = f32[8,8,1024]{2,1,0:T(8,128)} custom-call(f32[64,2048]{1,0:T(8,128)} %bitcast.7.refs_0_, f32[512,512]{1,0:T(8,128)S(1)} %get-tuple-element.7.refs_1_.refs_3_, f32[512,512]{1,0:T(8,128)S(1)} %collective-permute-done.refs_2_.refs_4_, f32[512,512]{1,0:T(8,128)S(1)} %collective-permute-done.1.refs_3_.refs_5_, ...), custom_call_target="tpu_custom_call" | custom-call | tf_op jit(solution)/shard_map/pallas_call | solution.py:105
  110.0 3.6 %all-to-all-start.4 = ((f32[8,8,1024]{2,1,0:T(8,128)}), f32[8,8,1024]{2,1,0:T(8,128)S(1)}, u32[]{:S(2)}, u32[]{:S(2)}) async-start(f32[8,8,1024]{2,1,0:T(8,128)} %shard_map.64), calls=%async_computation.4 | async-start | bytes 524288 | tf_op jit(solution)/shard_map/all_to_all | solution.py:19
  113.6 9.0 %collective-permute-done.7.refs_0_ = f32[64,2048]{1,0:T(8,128)} collective-permute-done((f32[64,2048]{1,0:T(8,128)}, f32[64,2048]{1,0:T(8,128)}, u32[]{:S(2)}, u32[]{:S(2)}) %collective-permute-start.7) | collective-permute-done | bytes 524320 | tf_op jit(solution)/shard_map/ppermute | solution.py:15
  122.6 3.7 %collective-permute-done.9.refs_2_ = f32[64,2048]{1,0:T(8,128)} collective-permute-done((f32[64,2048]{1,0:T(8,128)}, f32[64,2048]{1,0:T(8,128)}, u32[]{:S(2)}, u32[]{:S(2)}) %collective-permute-start.9) | collective-permute-done | bytes 524320 | tf_op jit(solution)/shard_map/ppermute | solution.py:15
  126.3 5.6 %shard_map.65 = f32[8,24,1024]{2,1,0:T(8,128)S(1)} custom-call(f32[64,2048]{1,0:T(8,128)} %collective-permute-done.7.refs_0_, f32[64,2048]{1,0:T(8,128)} %collective-permute-done.8.refs_1_, f32[64,2048]{1,0:T(8,128)} %collective-permute-done.9.refs_2_, f32[512,512]{1,0:T(8,128)S(1)} %get-tuple-element.7.refs_1_.refs_3_, ...), custom_call_target="tpu_custom_call" | custom-call | tf_op jit(solution)/shard_map/pallas_call | solution.py:105
  132.8 4.3 %all-to-all-start.5 = ((f32[8,24,1024]{2,1,0:T(8,128)}), f32[8,24,1024]{2,1,0:T(8,128)S(1)}, u32[]{:S(2)}, u32[]{:S(2)}) async-start(f32[8,24,1024]{2,1,0:T(8,128)} %copy-done), calls=%async_computation.5 | async-start | bytes 1572864 | tf_op jit(solution)/shard_map/all_to_all | solution.py:19
  137.1 23.3 %all-to-all-done.5.second_ref = f32[8,24,1024]{2,1,0:T(8,128)S(1)} async-done(((f32[8,24,1024]{2,1,0:T(8,128)}), f32[8,24,1024]{2,1,0:T(8,128)S(1)}, u32[]{:S(2)}, u32[]{:S(2)}) %all-to-all-start.5) | async-done | bytes 786464 | tf_op jit(solution)/shard_map/all_to_all | solution.py:19
  161.5 3.6 %all-to-all-start.6 = ((f32[8,32,1024]{2,1,0:T(8,128)}), f32[8,32,1024]{2,1,0:T(8,128)S(1)}, u32[]{:S(2)}, u32[]{:S(2)}) async-start(f32[8,32,1024]{2,1,0:T(8,128)} %sum_copies.1), calls=%async_computation.6 | async-start | bytes 2097152 | tf_op jit(solution)/shard_map/all_to_all | solution.py:19
  166.7 2.1 collective-permute-start.10
  170.3 21.2 %collective-permute-done.10.refs_2_ = f32[256,512]{1,0:T(8,128)S(1)} collective-permute-done((f32[256,512]{1,0:T(8,128)S(1)}, f32[256,512]{1,0:T(8,128)S(1)}, u32[]{:S(2)}, u32[]{:S(2)}) %collective-permute-start.10) | collective-permute-done | bytes 524320 | tf_op jit(solution)/shard_map/ppermute | solution.py:15
  192.0 3.0 %collective-permute-done.12.refs_4_ = f32[256,512]{1,0:T(8,128)S(1)} collective-permute-done((f32[256,512]{1,0:T(8,128)S(1)}, f32[256,512]{1,0:T(8,128)S(1)}, u32[]{:S(2)}, u32[]{:S(2)}) %collective-permute-start.12) | collective-permute-done | bytes 524320 | tf_op jit(solution)/shard_map/ppermute | solution.py:15
  204.3 19.6 %all_to_all.42 = f32[16,64,256]{2,1,0:T(8,128)S(1)} all-to-all(f32[16,64,256]{2,1,0:T(8,128)S(1)} %score.1), channel_id=1, replica_groups=mesh['y'=4,'core'=2,'z'=8,'x'=4] {'y','x'}, dimensions={0} | all-to-all | bytes 2097152 | tf_op jit(solution)/shard_map/all_to_all | solution.py:19
  (66 shorter events, 22.9 us)
Async XLA Ops:
  0.0 1.5 copy-start.1
  6.7 20.9 %all-to-all-start = ((f32[4,256,256]{2,1,0:T(8,128)}), f32[4,256,256]{2,1,0:T(8,128)}, u32[]{:S(2)}, u32[]{:S(2)}) async-start(f32[4,256,256]{2,1,0:T(8,128)} %bitcast.2), calls=%async_computation | async-start | bytes 2097152 | tf_op jit(solution)/shard_map/all_to_all | solution.py:19
  17.0 32.3 %collective-permute-start = (f32[512,512]{1,0:T(8,128)}, f32[512,512]{1,0:T(8,128)S(1)}, u32[]{:S(2)}, u32[]{:S(2)}) collective-permute-start(f32[512,512]{1,0:T(8,128)} %get-tuple-element.6), channel_id=1, source_target_pairs={{0,1},{1,2},{2,3},{3,0},{4,5},{5,6},{6,7},{7,4},{8,9},{9,10},{10,1... | collective-permute-start | bytes 3145736 | tf_op jit(solution)/shard_map/ppermute | solution.py:15
  17.1 32.9 %collective-permute-start.1 = (f32[512,512]{1,0:T(8,128)}, f32[512,512]{1,0:T(8,128)S(1)}, u32[]{:S(2)}, u32[]{:S(2)}) collective-permute-start(f32[512,512]{1,0:T(8,128)} %get-tuple-element.8), channel_id=1, source_target_pairs={{0,2},{1,3},{2,0},{3,1},{4,6},{5,7},{6,4},{7,5},{8,10},{9,11},{10,... | collective-permute-start | bytes 3145736 | tf_op jit(solution)/shard_map/ppermute | solution.py:15
  20.0 49.2 %collective-permute-start.2 = (f32[512,512]{1,0:T(8,128)}, f32[512,512]{1,0:T(8,128)}, u32[]{:S(2)}, u32[]{:S(2)}) collective-permute-start(f32[512,512]{1,0:T(8,128)} %get-tuple-element.5), channel_id=1, source_target_pairs={{0,3},{1,0},{2,1},{3,2},{4,7},{5,4},{6,5},{7,6},{8,11},{9,8},{10,9... | collective-permute-start | bytes 3145736 | tf_op jit(solution)/shard_map/ppermute | solution.py:15
  29.6 39.5 %all-to-all-start.1 = ((f32[8,32,256]{2,1,0:T(8,128)}), f32[8,32,256]{2,1,0:T(8,128)S(1)}, u32[]{:S(2)}, u32[]{:S(2)}) async-start(f32[8,32,256]{2,1,0:T(8,128)} %bitcast.3), calls=%async_computation.1 | async-start | bytes 524288 | tf_op jit(solution)/shard_map/all_to_all | solution.py:19
  36.6 66.1 %collective-permute-start.3 = (f32[512,512]{1,0:T(8,128)S(1)}, f32[512,512]{1,0:T(8,128)}, u32[]{:S(2)}, u32[]{:S(2)}) collective-permute-start(f32[512,512]{1,0:T(8,128)S(1)} %get-tuple-element.7.refs_1_.refs_3_), channel_id=1, source_target_pairs={{0,32},{32,0},{1,33},{33,1},{2,34},{34,2},{3,35},{35,3},{4,36},{36... | collective-permute-start | bytes 3145736 | tf_op jit(solution)/shard_map/ppermute | solution.py:181
  49.3 53.9 %collective-permute-start.4 = (f32[512,512]{1,0:T(8,128)S(1)}, f32[512,512]{1,0:T(8,128)}, u32[]{:S(2)}, u32[]{:S(2)}) collective-permute-start(f32[512,512]{1,0:T(8,128)S(1)} %collective-permute-done.refs_2_.refs_4_), channel_id=1, source_target_pairs={{0,32},{32,0},{1,33},{33,1},{2,34},{34,2},{3,35},{35,3},{4,36},{36... | collective-permute-start | bytes 3145736 | tf_op jit(solution)/shard_map/ppermute | solution.py:181
  50.0 54.3 %collective-permute-start.5 = (f32[512,512]{1,0:T(8,128)S(1)}, f32[512,512]{1,0:T(8,128)}, u32[]{:S(2)}, u32[]{:S(2)}) collective-permute-start(f32[512,512]{1,0:T(8,128)S(1)} %collective-permute-done.1.refs_3_.refs_5_), channel_id=1, source_target_pairs={{0,32},{32,0},{1,33},{33,1},{2,34},{34,2},{3,35},{35,3},{4,36},{36... | collective-permute-start | bytes 3145736 | tf_op jit(solution)/shard_map/ppermute | solution.py:181
  69.1 35.1 %collective-permute-start.6 = (f32[512,512]{1,0:T(8,128)}, f32[512,512]{1,0:T(8,128)}, u32[]{:S(2)}, u32[]{:S(2)}) collective-permute-start(f32[512,512]{1,0:T(8,128)} %collective-permute-done.2.refs_4_.refs_6_), channel_id=1, source_target_pairs={{0,32},{32,0},{1,33},{33,1},{2,34},{34,2},{3,35},{35,3},{4,36},{36... | collective-permute-start | bytes 3145736 | tf_op jit(solution)/shard_map/ppermute | solution.py:181
  99.6 23.0 %collective-permute-start.7 = (f32[64,2048]{1,0:T(8,128)}, f32[64,2048]{1,0:T(8,128)}, u32[]{:S(2)}, u32[]{:S(2)}) collective-permute-start(f32[64,2048]{1,0:T(8,128)} %bitcast.7.refs_0_), channel_id=1, source_target_pairs={{0,192},{64,0},{128,64},{192,128},{1,193},{65,1},{129,65},{193,129... | collective-permute-start | bytes 1572872 | tf_op jit(solution)/shard_map/ppermute | solution.py:15
  102.6 20.0 %collective-permute-start.8 = (f32[64,2048]{1,0:T(8,128)}, f32[64,2048]{1,0:T(8,128)}, u32[]{:S(2)}, u32[]{:S(2)}) collective-permute-start(f32[64,2048]{1,0:T(8,128)} %bitcast.7.refs_0_), channel_id=1, source_target_pairs={{0,128},{64,192},{128,0},{192,64},{1,129},{65,193},{129,1},{193,65... | collective-permute-start | bytes 1572872 | tf_op jit(solution)/shard_map/ppermute | solution.py:15
  103.3 23.0 %collective-permute-start.9 = (f32[64,2048]{1,0:T(8,128)}, f32[64,2048]{1,0:T(8,128)}, u32[]{:S(2)}, u32[]{:S(2)}) collective-permute-start(f32[64,2048]{1,0:T(8,128)} %bitcast.7.refs_0_), channel_id=1, source_target_pairs={{0,64},{64,128},{128,192},{192,0},{1,65},{65,129},{129,193},{193,1... | collective-permute-start | bytes 1572872 | tf_op jit(solution)/shard_map/ppermute | solution.py:15
  110.0 22.8 %all-to-all-start.4 = ((f32[8,8,1024]{2,1,0:T(8,128)}), f32[8,8,1024]{2,1,0:T(8,128)S(1)}, u32[]{:S(2)}, u32[]{:S(2)}) async-start(f32[8,8,1024]{2,1,0:T(8,128)} %shard_map.64), calls=%async_computation.4 | async-start | bytes 524288 | tf_op jit(solution)/shard_map/all_to_all | solution.py:19
  132.8 27.6 %all-to-all-start.5 = ((f32[8,24,1024]{2,1,0:T(8,128)}), f32[8,24,1024]{2,1,0:T(8,128)S(1)}, u32[]{:S(2)}, u32[]{:S(2)}) async-start(f32[8,24,1024]{2,1,0:T(8,128)} %copy-done), calls=%async_computation.5 | async-start | bytes 1572864 | tf_op jit(solution)/shard_map/all_to_all | solution.py:19
  161.5 36.8 %all-to-all-start.6 = ((f32[8,32,1024]{2,1,0:T(8,128)}), f32[8,32,1024]{2,1,0:T(8,128)S(1)}, u32[]{:S(2)}, u32[]{:S(2)}) async-start(f32[8,32,1024]{2,1,0:T(8,128)} %sum_copies.1), calls=%async_computation.6 | async-start | bytes 2097152 | tf_op jit(solution)/shard_map/all_to_all | solution.py:19
  166.7 24.8 %collective-permute-start.10 = (f32[256,512]{1,0:T(8,128)S(1)}, f32[256,512]{1,0:T(8,128)S(1)}, u32[]{:S(2)}, u32[]{:S(2)}) collective-permute-start(f32[256,512]{1,0:T(8,128)S(1)} %get-tuple-element.10), channel_id=1, source_target_pairs={{0,1},{1,2},{2,3},{3,0},{4,5},{5,6},{6,7},{7,4},{8,9},{9,10},{10,1... | collective-permute-start | bytes 1572872 | tf_op jit(solution)/shard_map/ppermute | solution.py:15
  168.9 22.6 %collective-permute-start.11 = (f32[256,512]{1,0:T(8,128)S(1)}, f32[256,512]{1,0:T(8,128)S(1)}, u32[]{:S(2)}, u32[]{:S(2)}) collective-permute-start(f32[256,512]{1,0:T(8,128)S(1)} %get-tuple-element.12), channel_id=1, source_target_pairs={{0,2},{1,3},{2,0},{3,1},{4,6},{5,7},{6,4},{7,5},{8,10},{9,11},{10,... | collective-permute-start | bytes 1572872 | tf_op jit(solution)/shard_map/ppermute | solution.py:15
  169.0 26.0 %collective-permute-start.12 = (f32[256,512]{1,0:T(8,128)S(1)}, f32[256,512]{1,0:T(8,128)S(1)}, u32[]{:S(2)}, u32[]{:S(2)}) collective-permute-start(f32[256,512]{1,0:T(8,128)S(1)} %get-tuple-element.9), channel_id=1, source_target_pairs={{0,3},{1,0},{2,1},{3,2},{4,7},{5,4},{6,5},{7,6},{8,11},{9,8},{10,9... | collective-permute-start | bytes 1572872 | tf_op jit(solution)/shard_map/ppermute | solution.py:15
  170.3 24.7 %collective-permute-start.13 = (f32[256,512]{1,0:T(8,128)S(1)}, f32[256,512]{1,0:T(8,128)S(1)}, u32[]{:S(2)}, u32[]{:S(2)}) collective-permute-start(f32[256,512]{1,0:T(8,128)S(1)} %get-tuple-element.11.refs_1_), channel_id=1, source_target_pairs={{0,32},{32,0},{1,33},{33,1},{2,34},{34,2},{3,35},{35,3},{4,36},{36... | collective-permute-start | bytes 1572872 | tf_op jit(solution)/shard_map/ppermute | solution.py:181
  191.5 4.3 %collective-permute-start.14 = (f32[256,512]{1,0:T(8,128)S(1)}, f32[256,512]{1,0:T(8,128)S(1)}, u32[]{:S(2)}, u32[]{:S(2)}) collective-permute-start(f32[256,512]{1,0:T(8,128)S(1)} %collective-permute-done.10.refs_2_), channel_id=1, source_target_pairs={{0,32},{32,0},{1,33},{33,1},{2,34},{34,2},{3,35},{35,3},{4,36},{36... | collective-permute-start | bytes 1572872 | tf_op jit(solution)/shard_map/ppermute | solution.py:181
  191.5 5.1 %collective-permute-start.15 = (f32[256,512]{1,0:T(8,128)S(1)}, f32[256,512]{1,0:T(8,128)S(1)}, u32[]{:S(2)}, u32[]{:S(2)}) collective-permute-start(f32[256,512]{1,0:T(8,128)S(1)} %collective-permute-done.11.refs_3_), channel_id=1, source_target_pairs={{0,32},{32,0},{1,33},{33,1},{2,34},{34,2},{3,35},{35,3},{4,36},{36... | collective-permute-start | bytes 1572872 | tf_op jit(solution)/shard_map/ppermute | solution.py:181
  195.0 2.4 %collective-permute-start.16 = (f32[256,512]{1,0:T(8,128)S(1)}, f32[256,512]{1,0:T(8,128)S(1)}, u32[]{:S(2)}, u32[]{:S(2)}) collective-permute-start(f32[256,512]{1,0:T(8,128)S(1)} %collective-permute-done.12.refs_4_), channel_id=1, source_target_pairs={{0,32},{32,0},{1,33},{33,1},{2,34},{34,2},{3,35},{35,3},{4,36},{36... | collective-permute-start | bytes 1572872 | tf_op jit(solution)/shard_map/ppermute | solution.py:181
  198.2 1.0 copy-start.4
  (11 other events, 10.1 us)

commit v3 on v2

--- a/solution.py
+++ b/solution.py
@@ -71,7 +71,6 @@
         out_specs=pl.BlockSpec((rows, columns), lambda i: (i, 0)),
         out_shape=jax.ShapeDtypeStruct((inputs.shape[0], columns), f32),
         name="project",
-        compiler_params=ROOM,
     )(inputs, out_grads, proj_in, proj_out)
 
 
@@ -111,23 +110,22 @@
     )(*[near(g) for g in owned], *[near(f) for f in fisher[0] + fisher[1]])
 
 
-def sum_copies(first, second):
-    few, columns = first.shape
-    nz, many = second.shape[:2]
-
-    def kernel(first_ref, second_ref, out_ref):
-        total = jnp.concatenate([first_ref[...], jnp.sum(second_ref[...], axis=0)], axis=0)
+def sum_copies(pieces):
+    nz = pieces.shape[0]
+
+    def kernel(pieces_ref, out_ref):
+        total = jnp.sum(pieces_ref[...], axis=0)
         for z in range(nz):
             out_ref[z] = total
 
     return pl.pallas_call(
         kernel,
-        in_specs=[WHOLE] * 2,
+        in_specs=[WHOLE],
         out_specs=WHOLE,
-        out_shape=pltpu.VMEM((nz, few + many, columns), f32),
+        out_shape=pltpu.VMEM(pieces.shape, f32),
         name="sum_copies",
         compiler_params=ROOM,
-    )(near(first), near(second))
+    )(near(pieces))
 
 
 def score(whole, stored, ny):
@@ -201,11 +199,8 @@
     owned = []
     for d in range(ny):
         owned.append(shifted(mine, "y", ny, -d))
-    ahead = precondition(owned[:1], fisher, nz)
-    ahead = summed(pieces_of(ahead, "z"))
-    rest = precondition(owned[1:], fisher, nz)
-    rest = pieces_of(rest, "z")
-    whole = pieces_of(sum_copies(ahead, rest), "z")
+    part = pieces_of(precondition(owned, fisher, nz), "z")
+    whole = pieces_of(sum_copies(part), "z")
     scores = pieces_of(score(whole, stored, ny), ("y", "x"))
     return jnp.sum(scores, axis=0)
 

time: 228 us -> 228 us (level)
  blocking collectives: 49.4 us -> 81.6 us
  waiting for transfers between devices: 100 us -> 76.9 us
  local copies, waits for them, and re-layouts: 18.6 us -> 13.9 us
  Pallas kernels: 16.6 us -> 13.2 us
    all_to_all x3, blocking collectives: 49.4 us -> 81.6 us  [pieces_of(): return lax.all_to_all(array, axis, 0, 0)]
    all_to_all x5 -> x4, waiting for transfers between devices: 30.9 us -> 7.67 us  [pieces_of(): return lax.all_to_all(array, axis, 0, 0)]
    pallas_call x2 -> x1, Pallas kernels: 11.4 us -> 5.94 us  [precondition(): pl.pallas_call(kernel, in_specs=[WHOLE] * (count + 2 * nx), out_specs=WHO...]
    unnamed x26 -> x16, local copies, waits for them, and re-layouts: 12.6 us -> 7.35 us
    all_to_all x5 -> x4, starting transfers between devices: 24.8 us -> 23.8 us  [pieces_of(): return lax.all_to_all(array, axis, 0, 0)]
  transfers between devices with their start and end apart: 22 -> 21, of which waited for: 9 -> 7; matrix products, arithmetic and copies ran while one was open for 4% -> 4% of each run, Pallas kernels for 5% -> 0%
where the time goes in v3:
time: 228 us; the launch traced here: 225 us
  blocking collectives  81.6 us (36%)
  waiting for transfers between devices  76.9 us (34%)
  starting transfers between devices  35.9 us (16%)
  local copies, waits for them, and re-layouts  13.9 us (6%)
  Pallas kernels  13.2 us (6%)
  other arithmetic  2.74 us (1%)
    all_to_all x3, blocking collectives, pieces_of(): return lax.all_to_all(array, axis, 0, 0)  81.6 us
    ppermute x9, waiting for transfers between devices, shifted(): lax.ppermute(array, axis, [(i, (i + steps) % size) for i in range(size)])  69.2 us
    all_to_all x4, starting transfers between devices, pieces_of(): return lax.all_to_all(array, axis, 0, 0)  23.8 us
    ppermute x9, starting transfers between devices, shifted(): lax.ppermute(array, axis, [(i, (i + steps) % size) for i in range(size)])  11.3 us
    all_to_all x4, waiting for transfers between devices, pieces_of(): return lax.all_to_all(array, axis, 0, 0)  7.67 us
    unnamed x16, local copies, waits for them, and re-layouts  7.35 us
    pallas_call x1, Pallas kernels, precondition(): pl.pallas_call(kernel, in_specs=[WHOLE] * (count + 2 * nx), out_specs=WHO...  5.94 us
    dynamic_slice x2, local copies, waits for them, and re-layouts, spread(): piece = lax.dynamic_slice_in_dim(array, (x + k & nx - 1) * width, width, 1)  5.67 us
  transfers between devices with their start and end apart: 21, of which 7 were waited for; matrix products, arithmetic and copies ran while one was open for 4% of the time, Pallas kernels for 0%

profile of v3, /device:TPU:6, one launch (start us, length us, event | category | flops | bytes accessed | tf_op | source)
XLA Modules:
  0.0 224.7 jit_solution(17214048737882535413)
XLA Ops:
  0.0 4.3 %project.1 = f32[1024,256]{1,0:T(8,128)} custom-call(bf16[1024,896]{1,0:T(8,128)(2,1)} %bitcast.17, bf16[1024,256]{1,0:T(8,128)(2,1)} %bitcast.18, bf16[896,128]{1,0:T(8,128)(2,1)} %proj_in_ref.1, bf16[256,128]{1,0:T(8,128)(2,1)} %proj_out_ref.1), custom_call_target="tpu_custom_call" | custom-call | tf_op jit(solution)/shard_map/project/pallas_call | solution.py:67
  4.3 6.4 %all-to-all-start = ((f32[4,256,256]{2,1,0:T(8,128)}), f32[4,256,256]{2,1,0:T(8,128)}, u32[]{:S(2)}, u32[]{:S(2)}) async-start(f32[4,256,256]{2,1,0:T(8,128)} %bitcast.16), calls=%async_computation | async-start | bytes 2097152 | tf_op jit(solution)/shard_map/all_to_all | solution.py:19
  10.7 4.0 %constant_dynamic-slice_fusion.4 = (f32[512,512]{1,0:T(8,128)}, f32[512,512]{1,0:T(8,128)}, f32[512,512]{1,0:T(8,128)S(1)}, f32[512,512]{1,0:T(8,128)}) fusion(f32[512,2048]{1,0:T(8,128)} %param.10, s32[]{:T(128)S(6)} %select_n.19, s32[]{:T(128)S(6)} %select_n.17, s32[]{:T(128)S(6)} %select_n.16, s32[]{:T(128)S(6)} %select_n.18), kind=kLoop, calls=%fused_computation.5 | loop fusion | bytes 8388624 | tf_op jit(solution)/shard_map/dynamic_slice | solution.py:176
  14.7 2.9 %collective-permute-start.4 = (f32[512,512]{1,0:T(8,128)}, f32[512,512]{1,0:T(8,128)S(1)}, u32[]{:S(2)}, u32[]{:S(2)}) collective-permute-start(f32[512,512]{1,0:T(8,128)} %get-tuple-element.8), channel_id=1, source_target_pairs={{0,2},{1,3},{2,0},{3,1},{4,6},{5,7},{6,4},{7,5},{8,10},{9,11},{10,... | collective-permute-start | bytes 3145736 | tf_op jit(solution)/shard_map/ppermute | solution.py:15
  17.6 7.7 %all-to-all-done = f32[4,256,256]{2,1,0:T(8,128)} async-done(((f32[4,256,256]{2,1,0:T(8,128)}), f32[4,256,256]{2,1,0:T(8,128)}, u32[]{:S(2)}, u32[]{:S(2)}) %all-to-all-start) | async-done | bytes 1048608 | tf_op jit(solution)/shard_map/all_to_all | solution.py:19
  25.2 2.0 reduce_sum.27
  27.3 6.9 %all-to-all-start.1 = ((f32[8,32,256]{2,1,0:T(8,128)}), f32[8,32,256]{2,1,0:T(8,128)S(1)}, u32[]{:S(2)}, u32[]{:S(2)}) async-start(f32[8,32,256]{2,1,0:T(8,128)} %bitcast.3), calls=%async_computation.1 | async-start | bytes 524288 | tf_op jit(solution)/shard_map/all_to_all | solution.py:19
  34.2 12.8 %collective-permute-done.3.refs_5_ = f32[512,512]{1,0:T(8,128)S(1)} collective-permute-done((f32[512,512]{1,0:T(8,128)}, f32[512,512]{1,0:T(8,128)S(1)}, u32[]{:S(2)}, u32[]{:S(2)}) %collective-permute-start.3) | collective-permute-done | bytes 1048608 | tf_op jit(solution)/shard_map/ppermute | solution.py:15
  48.2 6.9 %all-to-all-start.2 = ((f32[8,2,2048]{2,1,0:T(2,128)}), f32[8,2,2048]{2,1,0:T(2,128)S(1)}, u32[]{:S(2)}, u32[]{:S(2)}) async-start(f32[8,2,2048]{2,1,0:T(2,128)} %bitcast.11), calls=%async_computation.2 | async-start | bytes 262144 | tf_op jit(solution)/shard_map/all_to_all | solution.py:19
  55.4 11.3 %collective-permute-done.5.refs_7_ = f32[512,512]{1,0:T(8,128)} collective-permute-done((f32[512,512]{1,0:T(8,128)}, f32[512,512]{1,0:T(8,128)}, u32[]{:S(2)}, u32[]{:S(2)}) %collective-permute-start.5) | collective-permute-done | bytes 1048608 | tf_op jit(solution)/shard_map/ppermute | solution.py:15
  66.8 30.2 %all_to_all.35 = f32[4,16,2048]{2,1,0:T(8,128)S(1)} all-to-all(f32[4,16,2048]{2,1,0:T(8,128)S(1)} %broadcast_in_dim.8), channel_id=1, replica_groups=mesh['y'=4,'core'=2,'z'=8,'x'=4] {'x'}, dimensions={0} | all-to-all | bytes 1048576 | tf_op jit(solution)/shard_map/all_to_all | solution.py:19
  97.0 3.0 %collective-permute-start = (f32[64,2048]{1,0:T(8,128)S(1)}, f32[64,2048]{1,0:T(8,128)S(1)}, u32[]{:S(2)}, u32[]{:S(2)}) collective-permute-start(f32[64,2048]{1,0:T(8,128)S(1)} %bitcast.12), channel_id=1, source_target_pairs={{0,192},{64,0},{128,64},{192,128},{1,193},{65,1},{129,65},{193,129... | collective-permute-start | bytes 1572872 | tf_op jit(solution)/shard_map/ppermute | solution.py:15
  101.6 18.8 %collective-permute-done.refs_1_ = f32[64,2048]{1,0:T(8,128)S(1)} collective-permute-done((f32[64,2048]{1,0:T(8,128)S(1)}, f32[64,2048]{1,0:T(8,128)S(1)}, u32[]{:S(2)}, u32[]{:S(2)}) %collective-permute-start) | collective-permute-done | bytes 524320 | tf_op jit(solution)/shard_map/ppermute | solution.py:15
  120.4 3.7 %collective-permute-done.2.refs_3_ = f32[64,2048]{1,0:T(8,128)S(1)} collective-permute-done((f32[64,2048]{1,0:T(8,128)S(1)}, f32[64,2048]{1,0:T(8,128)S(1)}, u32[]{:S(2)}, u32[]{:S(2)}) %collective-permute-start.2) | collective-permute-done | bytes 524320 | tf_op jit(solution)/shard_map/ppermute | solution.py:15
  124.1 5.9 %shard_map.64 = f32[8,32,1024]{2,1,0:T(8,128)S(1)} custom-call(f32[64,2048]{1,0:T(8,128)S(1)} %bitcast.15, f32[64,2048]{1,0:T(8,128)S(1)} %collective-permute-done.refs_1_, f32[64,2048]{1,0:T(8,128)S(1)} %collective-permute-done.1.refs_2_, f32[64,2048]{1,0:T(8,128)S(1)} %collective-permute-done.2.refs_3_, f32[512,512]{1,0:T(8,128)S(1)} %get-tuple-element.7.refs_4_, ...), custom_call_target="tpu_custom_call" | custom-call | tf_op jit(solution)/shard_map/pallas_call | solution.py:104
  130.1 31.8 %all_to_all.36.pieces_ref = f32[8,32,1024]{2,1,0:T(8,128)S(1)} all-to-all(f32[8,32,1024]{2,1,0:T(8,128)S(1)} %shard_map.64), channel_id=1, replica_groups=mesh['y'=4,'core'=2,'z'=8,'x'=4] {'z'}, dimensions={0} | all-to-all | bytes 2097152 | tf_op jit(solution)/shard_map/all_to_all | solution.py:19
  163.0 3.6 %all-to-all-start.5 = ((f32[8,32,1024]{2,1,0:T(8,128)}), f32[8,32,1024]{2,1,0:T(8,128)S(1)}, u32[]{:S(2)}, u32[]{:S(2)}) async-start(f32[8,32,1024]{2,1,0:T(8,128)} %sum_copies.1), calls=%async_computation.5 | async-start | bytes 2097152 | tf_op jit(solution)/shard_map/all_to_all | solution.py:19
  166.6 1.7 constant_dynamic-slice_fusion
  168.3 2.3 %collective-permute-start.10 = (f32[256,512]{1,0:T(8,128)S(1)}, f32[256,512]{1,0:T(8,128)S(1)}, u32[]{:S(2)}, u32[]{:S(2)}) collective-permute-start(f32[256,512]{1,0:T(8,128)S(1)} %get-tuple-element.10), channel_id=1, source_target_pairs={{0,1},{1,2},{2,3},{3,0},{4,5},{5,6},{6,7},{7,4},{8,9},{9,10},{10,1... | collective-permute-start | bytes 1572872 | tf_op jit(solution)/shard_map/ppermute | solution.py:15
  170.8 1.3 collective-permute-start.12
  172.1 19.6 %collective-permute-done.10.refs_2_ = f32[256,512]{1,0:T(8,128)S(1)} collective-permute-done((f32[256,512]{1,0:T(8,128)S(1)}, f32[256,512]{1,0:T(8,128)S(1)}, u32[]{:S(2)}, u32[]{:S(2)}) %collective-permute-start.10) | collective-permute-done | bytes 524320 | tf_op jit(solution)/shard_map/ppermute | solution.py:15
  192.2 3.0 %collective-permute-done.12.refs_4_ = f32[256,512]{1,0:T(8,128)S(1)} collective-permute-done((f32[256,512]{1,0:T(8,128)S(1)}, f32[256,512]{1,0:T(8,128)S(1)}, u32[]{:S(2)}, u32[]{:S(2)}) %collective-permute-start.12) | collective-permute-done | bytes 524320 | tf_op jit(solution)/shard_map/ppermute | solution.py:15
  202.6 1.9 score.1
  204.4 19.6 %all_to_all.37 = f32[16,64,256]{2,1,0:T(8,128)S(1)} all-to-all(f32[16,64,256]{2,1,0:T(8,128)S(1)} %score.1), channel_id=1, replica_groups=mesh['y'=4,'core'=2,'z'=8,'x'=4] {'y','x'}, dimensions={0} | all-to-all | bytes 2097152 | tf_op jit(solution)/shard_map/all_to_all | solution.py:19
  (52 shorter events, 13.1 us)
Async XLA Ops:
  4.3 21.0 %all-to-all-start = ((f32[4,256,256]{2,1,0:T(8,128)}), f32[4,256,256]{2,1,0:T(8,128)}, u32[]{:S(2)}, u32[]{:S(2)}) async-start(f32[4,256,256]{2,1,0:T(8,128)} %bitcast.16), calls=%async_computation | async-start | bytes 2097152 | tf_op jit(solution)/shard_map/all_to_all | solution.py:19
  14.6 32.3 %collective-permute-start.3 = (f32[512,512]{1,0:T(8,128)}, f32[512,512]{1,0:T(8,128)S(1)}, u32[]{:S(2)}, u32[]{:S(2)}) collective-permute-start(f32[512,512]{1,0:T(8,128)} %get-tuple-element.6), channel_id=1, source_target_pairs={{0,1},{1,2},{2,3},{3,0},{4,5},{5,6},{6,7},{7,4},{8,9},{9,10},{10,1... | collective-permute-start | bytes 3145736 | tf_op jit(solution)/shard_map/ppermute | solution.py:15
  14.7 40.4 %collective-permute-start.4 = (f32[512,512]{1,0:T(8,128)}, f32[512,512]{1,0:T(8,128)S(1)}, u32[]{:S(2)}, u32[]{:S(2)}) collective-permute-start(f32[512,512]{1,0:T(8,128)} %get-tuple-element.8), channel_id=1, source_target_pairs={{0,2},{1,3},{2,0},{3,1},{4,6},{5,7},{6,4},{7,5},{8,10},{9,11},{10,... | collective-permute-start | bytes 3145736 | tf_op jit(solution)/shard_map/ppermute | solution.py:15
  17.6 49.1 %collective-permute-start.5 = (f32[512,512]{1,0:T(8,128)}, f32[512,512]{1,0:T(8,128)}, u32[]{:S(2)}, u32[]{:S(2)}) collective-permute-start(f32[512,512]{1,0:T(8,128)} %get-tuple-element.5), channel_id=1, source_target_pairs={{0,3},{1,0},{2,1},{3,2},{4,7},{5,4},{6,5},{7,6},{8,11},{9,8},{10,9... | collective-permute-start | bytes 3145736 | tf_op jit(solution)/shard_map/ppermute | solution.py:15
  27.3 19.7 %all-to-all-start.1 = ((f32[8,32,256]{2,1,0:T(8,128)}), f32[8,32,256]{2,1,0:T(8,128)S(1)}, u32[]{:S(2)}, u32[]{:S(2)}) async-start(f32[8,32,256]{2,1,0:T(8,128)} %bitcast.3), calls=%async_computation.1 | async-start | bytes 524288 | tf_op jit(solution)/shard_map/all_to_all | solution.py:19
  34.2 65.9 %collective-permute-start.6 = (f32[512,512]{1,0:T(8,128)S(1)}, f32[512,512]{1,0:T(8,128)}, u32[]{:S(2)}, u32[]{:S(2)}) collective-permute-start(f32[512,512]{1,0:T(8,128)S(1)} %get-tuple-element.7.refs_4_), channel_id=1, source_target_pairs={{0,32},{32,0},{1,33},{33,1},{2,34},{34,2},{3,35},{35,3},{4,36},{36... | collective-permute-start | bytes 3145736 | tf_op jit(solution)/shard_map/ppermute | solution.py:179
  47.0 53.7 %collective-permute-start.7 = (f32[512,512]{1,0:T(8,128)S(1)}, f32[512,512]{1,0:T(8,128)}, u32[]{:S(2)}, u32[]{:S(2)}) collective-permute-start(f32[512,512]{1,0:T(8,128)S(1)} %collective-permute-done.3.refs_5_), channel_id=1, source_target_pairs={{0,32},{32,0},{1,33},{33,1},{2,34},{34,2},{3,35},{35,3},{4,36},{36... | collective-permute-start | bytes 3145736 | tf_op jit(solution)/shard_map/ppermute | solution.py:179
  48.2 18.5 %all-to-all-start.2 = ((f32[8,2,2048]{2,1,0:T(2,128)}), f32[8,2,2048]{2,1,0:T(2,128)S(1)}, u32[]{:S(2)}, u32[]{:S(2)}) async-start(f32[8,2,2048]{2,1,0:T(2,128)} %bitcast.11), calls=%async_computation.2 | async-start | bytes 262144 | tf_op jit(solution)/shard_map/all_to_all | solution.py:19
  55.1 46.6 %collective-permute-start.8 = (f32[512,512]{1,0:T(8,128)S(1)}, f32[512,512]{1,0:T(8,128)}, u32[]{:S(2)}, u32[]{:S(2)}) collective-permute-start(f32[512,512]{1,0:T(8,128)S(1)} %collective-permute-done.4.refs_6_), channel_id=1, source_target_pairs={{0,32},{32,0},{1,33},{33,1},{2,34},{34,2},{3,35},{35,3},{4,36},{36... | collective-permute-start | bytes 3145736 | tf_op jit(solution)/shard_map/ppermute | solution.py:179
  66.7 35.0 %collective-permute-start.9 = (f32[512,512]{1,0:T(8,128)}, f32[512,512]{1,0:T(8,128)}, u32[]{:S(2)}, u32[]{:S(2)}) collective-permute-start(f32[512,512]{1,0:T(8,128)} %collective-permute-done.5.refs_7_), channel_id=1, source_target_pairs={{0,32},{32,0},{1,33},{33,1},{2,34},{34,2},{3,35},{35,3},{4,36},{36... | collective-permute-start | bytes 3145736 | tf_op jit(solution)/shard_map/ppermute | solution.py:179
  97.0 23.4 %collective-permute-start = (f32[64,2048]{1,0:T(8,128)S(1)}, f32[64,2048]{1,0:T(8,128)S(1)}, u32[]{:S(2)}, u32[]{:S(2)}) collective-permute-start(f32[64,2048]{1,0:T(8,128)S(1)} %bitcast.12), channel_id=1, source_target_pairs={{0,192},{64,0},{128,64},{192,128},{1,193},{65,1},{129,65},{193,129... | collective-permute-start | bytes 1572872 | tf_op jit(solution)/shard_map/ppermute | solution.py:15
  100.0 20.4 %collective-permute-start.1 = (f32[64,2048]{1,0:T(8,128)S(1)}, f32[64,2048]{1,0:T(8,128)S(1)}, u32[]{:S(2)}, u32[]{:S(2)}) collective-permute-start(f32[64,2048]{1,0:T(8,128)S(1)} %bitcast.13), channel_id=1, source_target_pairs={{0,128},{64,192},{128,0},{192,64},{1,129},{65,193},{129,1},{193,65... | collective-permute-start | bytes 1572872 | tf_op jit(solution)/shard_map/ppermute | solution.py:15
  100.7 23.5 %collective-permute-start.2 = (f32[64,2048]{1,0:T(8,128)S(1)}, f32[64,2048]{1,0:T(8,128)S(1)}, u32[]{:S(2)}, u32[]{:S(2)}) collective-permute-start(f32[64,2048]{1,0:T(8,128)S(1)} %bitcast.14), channel_id=1, source_target_pairs={{0,64},{64,128},{128,192},{192,0},{1,65},{65,129},{129,193},{193,1... | collective-permute-start | bytes 1572872 | tf_op jit(solution)/shard_map/ppermute | solution.py:15
  163.0 35.4 %all-to-all-start.5 = ((f32[8,32,1024]{2,1,0:T(8,128)}), f32[8,32,1024]{2,1,0:T(8,128)S(1)}, u32[]{:S(2)}, u32[]{:S(2)}) async-start(f32[8,32,1024]{2,1,0:T(8,128)} %sum_copies.1), calls=%async_computation.5 | async-start | bytes 2097152 | tf_op jit(solution)/shard_map/all_to_all | solution.py:19
  168.3 23.4 %collective-permute-start.10 = (f32[256,512]{1,0:T(8,128)S(1)}, f32[256,512]{1,0:T(8,128)S(1)}, u32[]{:S(2)}, u32[]{:S(2)}) collective-permute-start(f32[256,512]{1,0:T(8,128)S(1)} %get-tuple-element.10), channel_id=1, source_target_pairs={{0,1},{1,2},{2,3},{3,0},{4,5},{5,6},{6,7},{7,4},{8,9},{9,10},{10,1... | collective-permute-start | bytes 1572872 | tf_op jit(solution)/shard_map/ppermute | solution.py:15
  170.7 21.1 %collective-permute-start.11 = (f32[256,512]{1,0:T(8,128)S(1)}, f32[256,512]{1,0:T(8,128)S(1)}, u32[]{:S(2)}, u32[]{:S(2)}) collective-permute-start(f32[256,512]{1,0:T(8,128)S(1)} %get-tuple-element.12), channel_id=1, source_target_pairs={{0,2},{1,3},{2,0},{3,1},{4,6},{5,7},{6,4},{7,5},{8,10},{9,11},{10,... | collective-permute-start | bytes 1572872 | tf_op jit(solution)/shard_map/ppermute | solution.py:15
  170.8 24.4 %collective-permute-start.12 = (f32[256,512]{1,0:T(8,128)S(1)}, f32[256,512]{1,0:T(8,128)S(1)}, u32[]{:S(2)}, u32[]{:S(2)}) collective-permute-start(f32[256,512]{1,0:T(8,128)S(1)} %get-tuple-element.9), channel_id=1, source_target_pairs={{0,3},{1,0},{2,1},{3,2},{4,7},{5,4},{6,5},{7,6},{8,11},{9,8},{10,9... | collective-permute-start | bytes 1572872 | tf_op jit(solution)/shard_map/ppermute | solution.py:15
  172.1 23.1 %collective-permute-start.13 = (f32[256,512]{1,0:T(8,128)S(1)}, f32[256,512]{1,0:T(8,128)S(1)}, u32[]{:S(2)}, u32[]{:S(2)}) collective-permute-start(f32[256,512]{1,0:T(8,128)S(1)} %get-tuple-element.11.refs_1_), channel_id=1, source_target_pairs={{0,32},{32,0},{1,33},{33,1},{2,34},{34,2},{3,35},{35,3},{4,36},{36... | collective-permute-start | bytes 1572872 | tf_op jit(solution)/shard_map/ppermute | solution.py:179
  191.7 4.3 %collective-permute-start.14 = (f32[256,512]{1,0:T(8,128)S(1)}, f32[256,512]{1,0:T(8,128)S(1)}, u32[]{:S(2)}, u32[]{:S(2)}) collective-permute-start(f32[256,512]{1,0:T(8,128)S(1)} %collective-permute-done.10.refs_2_), channel_id=1, source_target_pairs={{0,32},{32,0},{1,33},{33,1},{2,34},{34,2},{3,35},{35,3},{4,36},{36... | collective-permute-start | bytes 1572872 | tf_op jit(solution)/shard_map/ppermute | solution.py:179
  191.7 5.1 %collective-permute-start.15 = (f32[256,512]{1,0:T(8,128)S(1)}, f32[256,512]{1,0:T(8,128)S(1)}, u32[]{:S(2)}, u32[]{:S(2)}) collective-permute-start(f32[256,512]{1,0:T(8,128)S(1)} %collective-permute-done.11.refs_3_), channel_id=1, source_target_pairs={{0,32},{32,0},{1,33},{33,1},{2,34},{34,2},{3,35},{35,3},{4,36},{36... | collective-permute-start | bytes 1572872 | tf_op jit(solution)/shard_map/ppermute | solution.py:179
  195.2 2.4 %collective-permute-start.16 = (f32[256,512]{1,0:T(8,128)S(1)}, f32[256,512]{1,0:T(8,128)S(1)}, u32[]{:S(2)}, u32[]{:S(2)}) collective-permute-start(f32[256,512]{1,0:T(8,128)S(1)} %collective-permute-done.12.refs_4_), channel_id=1, source_target_pairs={{0,32},{32,0},{1,33},{33,1},{2,34},{34,2},{3,35},{35,3},{4,36},{36... | collective-permute-start | bytes 1572872 | tf_op jit(solution)/shard_map/ppermute | solution.py:179
  198.4 1.0 copy-start.1
  199.4 1.0 copy-start.3
  200.5 1.0 copy-start.5
  (5 other events, 4.2 us)

commit v4 on v3

--- a/solution.py
+++ b/solution.py
@@ -128,24 +128,37 @@
     )(near(pieces))
 
 
-def score(whole, stored, ny):
+def split_sides(whole, columns):
+    rows = whole.shape[0] * whole.shape[1]
+
+    def kernel(whole_ref, *out_refs):
+        for side in range(2):
+            values = whole_ref[:, :, side * columns : (side + 1) * columns].reshape(rows, columns)
+            out_refs[2 * side][...], out_refs[2 * side + 1][...] = halves(values)
+
+    return pl.pallas_call(
+        kernel,
+        in_specs=[WHOLE],
+        out_specs=[WHOLE] * 4,
+        out_shape=[pltpu.VMEM((rows, columns), bf16)] * 4,
+        name="split_sides",
+        compiler_params=ROOM,
+    )(near(whole))
+
+
+def score(left, stored, ny, nz):
     nx = len(stored[0])
-    many, columns = stored[0][0].shape
-    nz = whole.shape[0]
-    examples = nz * whole.shape[1] // ny
+    many = stored[0][0].shape[0]
+    examples = left[0].shape[0] // ny
 
     def kernel(*refs):
-        whole_ref, blocks = refs[0], refs[1 : 1 + 2 * nx]
-        out_ref = refs[1 + 2 * nx]
+        lefts, blocks, out_ref = refs[:4], refs[4 : 4 + 2 * nx], refs[4 + 2 * nx]
         x, y = lax.axis_index("x"), lax.axis_index("y")
-        left = []
-        for side in range(2):
-            values = whole_ref[:, :, side * columns : (side + 1) * columns]
-            left.append(halves(values.reshape(ny * examples, columns)))
         for k in range(nx):
             total = None
             for side in range(2):
-                term = product(left[side], halves(blocks[side * nx + k][...]), ((1,), (1,)))
+                pair = (lefts[2 * side][...], lefts[2 * side + 1][...])
+                term = product(pair, halves(blocks[side * nx + k][...]), ((1,), (1,)))
                 total = term if total is None else total + term
             total = total.reshape(nz, ny, examples // nz, many)
             for d in range(ny):
@@ -154,12 +167,12 @@
 
     return pl.pallas_call(
         kernel,
-        in_specs=[WHOLE] * (1 + 2 * nx),
+        in_specs=[WHOLE] * (4 + 2 * nx),
         out_specs=WHOLE,
         out_shape=pltpu.VMEM((ny * nx, examples, many), f32),
         name="score",
         compiler_params=ROOM,
-    )(near(whole), *[near(s) for s in stored[0] + stored[1]])
+    )(*[near(a) for a in left], *[near(s) for s in stored[0] + stored[1]])
 
 
 def on_device(sizes, inputs, out_grads, proj_in, proj_out, inv_fisher, store_grads):
@@ -201,7 +214,7 @@
         owned.append(shifted(mine, "y", ny, -d))
     part = pieces_of(precondition(owned, fisher, nz), "z")
     whole = pieces_of(sum_copies(part), "z")
-    scores = pieces_of(score(whole, stored, ny), ("y", "x"))
+    scores = pieces_of(score(split_sides(whole, width), stored, ny, nz), ("y", "x"))
     return jnp.sum(scores, axis=0)
 
 

time: 228 us -> 223 us (0.978)
  local copies, waits for them, and re-layouts: 13.9 us -> 6.59 us
    unnamed x16 -> x0, local copies, waits for them, and re-layouts: 7.35 us -> none
  transfers between devices with their start and end apart: 21 -> 21, of which waited for: 7 -> 8; matrix products, arithmetic and copies ran while one was open for 4% -> 4% of each run, Pallas kernels for 0% -> 0%
where the time goes in v4:
time: 223 us; the launch traced here: 221 us
  blocking collectives  81.3 us (36%)
  waiting for transfers between devices  78.7 us (35%)
  starting transfers between devices  35.9 us (16%)
  Pallas kernels  14.9 us (7%)
  local copies, waits for them, and re-layouts  6.59 us (3%)
  other arithmetic  2.74 us (1%)
    all_to_all x3, blocking collectives, pieces_of(): return lax.all_to_all(array, axis, 0, 0)  81.3 us
    ppermute x9, waiting for transfers between devices, shifted(): lax.ppermute(array, axis, [(i, (i + steps) % size) for i in range(size)])  69.2 us
    all_to_all x4, starting transfers between devices, pieces_of(): return lax.all_to_all(array, axis, 0, 0)  23.8 us
    ppermute x9, starting transfers between devices, shifted(): lax.ppermute(array, axis, [(i, (i + steps) % size) for i in range(size)])  11.3 us
    all_to_all x4, waiting for transfers between devices, pieces_of(): return lax.all_to_all(array, axis, 0, 0)  7.67 us
    pallas_call x1, Pallas kernels, precondition(): pl.pallas_call(kernel, in_specs=[WHOLE] * (count + 2 * nx), out_specs=WHO...  5.95 us
    dynamic_slice x2, local copies, waits for them, and re-layouts, spread(): piece = lax.dynamic_slice_in_dim(array, (x + k & nx - 1) * width, width, 1)  5.67 us
  transfers between devices with their start and end apart: 21, of which 8 were waited for; matrix products, arithmetic and copies ran while one was open for 4% of the time, Pallas kernels for 0%

profile of v4, /device:TPU:6, one launch (start us, length us, event | category | flops | bytes accessed | tf_op | source)
XLA Modules:
  0.0 220.6 jit_solution(10741123868169263568)
XLA Ops:
  0.0 4.3 %project.1 = f32[1024,256]{1,0:T(8,128)} custom-call(bf16[1024,896]{1,0:T(8,128)(2,1)} %bitcast.17, bf16[1024,256]{1,0:T(8,128)(2,1)} %bitcast.18, bf16[896,128]{1,0:T(8,128)(2,1)} %proj_in_ref.1, bf16[256,128]{1,0:T(8,128)(2,1)} %proj_out_ref.1), custom_call_target="tpu_custom_call" | custom-call | tf_op jit(solution)/shard_map/project/pallas_call | solution.py:67
  4.3 6.4 %all-to-all-start = ((f32[4,256,256]{2,1,0:T(8,128)}), f32[4,256,256]{2,1,0:T(8,128)}, u32[]{:S(2)}, u32[]{:S(2)}) async-start(f32[4,256,256]{2,1,0:T(8,128)} %bitcast.16), calls=%async_computation | async-start | bytes 2097152 | tf_op jit(solution)/shard_map/all_to_all | solution.py:19
  10.7 4.0 %constant_dynamic-slice_fusion.4 = (f32[512,512]{1,0:T(8,128)}, f32[512,512]{1,0:T(8,128)}, f32[512,512]{1,0:T(8,128)S(1)}, f32[512,512]{1,0:T(8,128)}) fusion(f32[512,2048]{1,0:T(8,128)} %param.10, s32[]{:T(128)S(6)} %select_n.19, s32[]{:T(128)S(6)} %select_n.17, s32[]{:T(128)S(6)} %select_n.16, s32[]{:T(128)S(6)} %select_n.18), kind=kLoop, calls=%fused_computation.5 | loop fusion | bytes 8388624 | tf_op jit(solution)/shard_map/dynamic_slice | solution.py:189
  14.7 2.9 %collective-permute-start.4 = (f32[512,512]{1,0:T(8,128)}, f32[512,512]{1,0:T(8,128)S(1)}, u32[]{:S(2)}, u32[]{:S(2)}) collective-permute-start(f32[512,512]{1,0:T(8,128)} %get-tuple-element.16), channel_id=1, source_target_pairs={{0,2},{1,3},{2,0},{3,1},{4,6},{5,7},{6,4},{7,5},{8,10},{9,11},{10,... | collective-permute-start | bytes 3145736 | tf_op jit(solution)/shard_map/ppermute | solution.py:15
  17.6 7.7 %all-to-all-done = f32[4,256,256]{2,1,0:T(8,128)} async-done(((f32[4,256,256]{2,1,0:T(8,128)}), f32[4,256,256]{2,1,0:T(8,128)}, u32[]{:S(2)}, u32[]{:S(2)}) %all-to-all-start) | async-done | bytes 1048608 | tf_op jit(solution)/shard_map/all_to_all | solution.py:19
  25.2 2.0 reduce_sum.27
  27.2 6.9 %all-to-all-start.1 = ((f32[8,32,256]{2,1,0:T(8,128)}), f32[8,32,256]{2,1,0:T(8,128)S(1)}, u32[]{:S(2)}, u32[]{:S(2)}) async-start(f32[8,32,256]{2,1,0:T(8,128)} %bitcast.3), calls=%async_computation.1 | async-start | bytes 524288 | tf_op jit(solution)/shard_map/all_to_all | solution.py:19
  34.2 12.8 %collective-permute-done.3.refs_5_ = f32[512,512]{1,0:T(8,128)S(1)} collective-permute-done((f32[512,512]{1,0:T(8,128)}, f32[512,512]{1,0:T(8,128)S(1)}, u32[]{:S(2)}, u32[]{:S(2)}) %collective-permute-start.3) | collective-permute-done | bytes 1048608 | tf_op jit(solution)/shard_map/ppermute | solution.py:15
  48.2 6.9 %all-to-all-start.2 = ((f32[8,2,2048]{2,1,0:T(2,128)}), f32[8,2,2048]{2,1,0:T(2,128)S(1)}, u32[]{:S(2)}, u32[]{:S(2)}) async-start(f32[8,2,2048]{2,1,0:T(2,128)} %bitcast.11), calls=%async_computation.2 | async-start | bytes 262144 | tf_op jit(solution)/shard_map/all_to_all | solution.py:19
  55.4 11.3 %collective-permute-done.5.refs_7_ = f32[512,512]{1,0:T(8,128)} collective-permute-done((f32[512,512]{1,0:T(8,128)}, f32[512,512]{1,0:T(8,128)}, u32[]{:S(2)}, u32[]{:S(2)}) %collective-permute-start.5) | collective-permute-done | bytes 1048608 | tf_op jit(solution)/shard_map/ppermute | solution.py:15
  66.9 30.1 %all_to_all.35 = f32[4,16,2048]{2,1,0:T(8,128)S(1)} all-to-all(f32[4,16,2048]{2,1,0:T(8,128)S(1)} %broadcast_in_dim.8), channel_id=1, replica_groups=mesh['y'=4,'core'=2,'z'=8,'x'=4] {'x'}, dimensions={0} | all-to-all | bytes 1048576 | tf_op jit(solution)/shard_map/all_to_all | solution.py:19
  97.0 3.0 %collective-permute-start = (f32[64,2048]{1,0:T(8,128)S(1)}, f32[64,2048]{1,0:T(8,128)S(1)}, u32[]{:S(2)}, u32[]{:S(2)}) collective-permute-start(f32[64,2048]{1,0:T(8,128)S(1)} %bitcast.12), channel_id=1, source_target_pairs={{0,192},{64,0},{128,64},{192,128},{1,193},{65,1},{129,65},{193,129... | collective-permute-start | bytes 1572872 | tf_op jit(solution)/shard_map/ppermute | solution.py:15
  101.6 18.8 %collective-permute-done.refs_1_ = f32[64,2048]{1,0:T(8,128)S(1)} collective-permute-done((f32[64,2048]{1,0:T(8,128)S(1)}, f32[64,2048]{1,0:T(8,128)S(1)}, u32[]{:S(2)}, u32[]{:S(2)}) %collective-permute-start) | collective-permute-done | bytes 524320 | tf_op jit(solution)/shard_map/ppermute | solution.py:15
  120.4 3.7 %collective-permute-done.2.refs_3_ = f32[64,2048]{1,0:T(8,128)S(1)} collective-permute-done((f32[64,2048]{1,0:T(8,128)S(1)}, f32[64,2048]{1,0:T(8,128)S(1)}, u32[]{:S(2)}, u32[]{:S(2)}) %collective-permute-start.2) | collective-permute-done | bytes 524320 | tf_op jit(solution)/shard_map/ppermute | solution.py:15
  124.1 5.9 %shard_map.64 = f32[8,32,1024]{2,1,0:T(8,128)S(1)} custom-call(f32[64,2048]{1,0:T(8,128)S(1)} %bitcast.15, f32[64,2048]{1,0:T(8,128)S(1)} %collective-permute-done.refs_1_, f32[64,2048]{1,0:T(8,128)S(1)} %collective-permute-done.1.refs_2_, f32[64,2048]{1,0:T(8,128)S(1)} %collective-permute-done.2.refs_3_, f32[512,512]{1,0:T(8,128)S(1)} %get-tuple-element.15.refs_4_, ...), custom_call_target="tpu_custom_call" | custom-call | tf_op jit(solution)/shard_map/pallas_call | solution.py:104
  130.1 31.8 %all_to_all.36.pieces_ref = f32[8,32,1024]{2,1,0:T(8,128)S(1)} all-to-all(f32[8,32,1024]{2,1,0:T(8,128)S(1)} %shard_map.64), channel_id=1, replica_groups=mesh['y'=4,'core'=2,'z'=8,'x'=4] {'z'}, dimensions={0} | all-to-all | bytes 2097152 | tf_op jit(solution)/shard_map/all_to_all | solution.py:19
  163.0 3.6 %all-to-all-start.5 = ((f32[8,32,1024]{2,1,0:T(8,128)}), f32[8,32,1024]{2,1,0:T(8,128)S(1)}, u32[]{:S(2)}, u32[]{:S(2)}) async-start(f32[8,32,1024]{2,1,0:T(8,128)} %sum_copies.1), calls=%async_computation.5 | async-start | bytes 2097152 | tf_op jit(solution)/shard_map/all_to_all | solution.py:19
  166.6 1.7 constant_dynamic-slice_fusion
  168.3 2.3 %collective-permute-start.10 = (f32[256,512]{1,0:T(8,128)S(1)}, f32[256,512]{1,0:T(8,128)S(1)}, u32[]{:S(2)}, u32[]{:S(2)}) collective-permute-start(f32[256,512]{1,0:T(8,128)S(1)} %get-tuple-element.18), channel_id=1, source_target_pairs={{0,1},{1,2},{2,3},{3,0},{4,5},{5,6},{6,7},{7,4},{8,9},{9,10},{10,1... | collective-permute-start | bytes 1572872 | tf_op jit(solution)/shard_map/ppermute | solution.py:15
  172.0 19.6 %collective-permute-done.10.refs_5_ = f32[256,512]{1,0:T(8,128)S(1)} collective-permute-done((f32[256,512]{1,0:T(8,128)S(1)}, f32[256,512]{1,0:T(8,128)S(1)}, u32[]{:S(2)}, u32[]{:S(2)}) %collective-permute-start.10) | collective-permute-done | bytes 524320 | tf_op jit(solution)/shard_map/ppermute | solution.py:15
  192.2 3.0 %collective-permute-done.12.refs_7_ = f32[256,512]{1,0:T(8,128)S(1)} collective-permute-done((f32[256,512]{1,0:T(8,128)S(1)}, f32[256,512]{1,0:T(8,128)S(1)}, u32[]{:S(2)}, u32[]{:S(2)}) %collective-permute-start.12) | collective-permute-done | bytes 524320 | tf_op jit(solution)/shard_map/ppermute | solution.py:15
  195.4 1.8 collective-permute-done.16.refs_11_
  197.2 3.4 %score.1 = f32[16,64,256]{2,1,0:T(8,128)S(1)} custom-call(bf16[256,512]{1,0:T(8,128)(2,1)S(1)} %get-tuple-element.9.refs_0_, bf16[256,512]{1,0:T(8,128)(2,1)S(1)} %get-tuple-element.10.refs_1_, bf16[256,512]{1,0:T(8,128)(2,1)S(1)} %get-tuple-element.11.refs_2_, bf16[256,512]{1,0:T(8,128)(2,1)S(1)} %get-tuple-element.12.refs_3_, ...), custom_call_target="tpu_custom_call" | custom-call | tf_op jit(solution)/shard_map/score/pallas_call | solution.py:168
  200.6 19.3 %all_to_all.37 = f32[16,64,256]{2,1,0:T(8,128)S(1)} all-to-all(f32[16,64,256]{2,1,0:T(8,128)S(1)} %score.1), channel_id=1, replica_groups=mesh['y'=4,'core'=2,'z'=8,'x'=4] {'y','x'}, dimensions={0} | all-to-all | bytes 2097152 | tf_op jit(solution)/shard_map/all_to_all | solution.py:19
  (37 shorter events, 7.2 us)
Async XLA Ops:
  4.3 20.9 %all-to-all-start = ((f32[4,256,256]{2,1,0:T(8,128)}), f32[4,256,256]{2,1,0:T(8,128)}, u32[]{:S(2)}, u32[]{:S(2)}) async-start(f32[4,256,256]{2,1,0:T(8,128)} %bitcast.16), calls=%async_computation | async-start | bytes 2097152 | tf_op jit(solution)/shard_map/all_to_all | solution.py:19
  14.6 32.3 %collective-permute-start.3 = (f32[512,512]{1,0:T(8,128)}, f32[512,512]{1,0:T(8,128)S(1)}, u32[]{:S(2)}, u32[]{:S(2)}) collective-permute-start(f32[512,512]{1,0:T(8,128)} %get-tuple-element.14), channel_id=1, source_target_pairs={{0,1},{1,2},{2,3},{3,0},{4,5},{5,6},{6,7},{7,4},{8,9},{9,10},{10,1... | collective-permute-start | bytes 3145736 | tf_op jit(solution)/shard_map/ppermute | solution.py:15
  14.7 40.4 %collective-permute-start.4 = (f32[512,512]{1,0:T(8,128)}, f32[512,512]{1,0:T(8,128)S(1)}, u32[]{:S(2)}, u32[]{:S(2)}) collective-permute-start(f32[512,512]{1,0:T(8,128)} %get-tuple-element.16), channel_id=1, source_target_pairs={{0,2},{1,3},{2,0},{3,1},{4,6},{5,7},{6,4},{7,5},{8,10},{9,11},{10,... | collective-permute-start | bytes 3145736 | tf_op jit(solution)/shard_map/ppermute | solution.py:15
  17.5 49.2 %collective-permute-start.5 = (f32[512,512]{1,0:T(8,128)}, f32[512,512]{1,0:T(8,128)}, u32[]{:S(2)}, u32[]{:S(2)}) collective-permute-start(f32[512,512]{1,0:T(8,128)} %get-tuple-element.13), channel_id=1, source_target_pairs={{0,3},{1,0},{2,1},{3,2},{4,7},{5,4},{6,5},{7,6},{8,11},{9,8},{10,9... | collective-permute-start | bytes 3145736 | tf_op jit(solution)/shard_map/ppermute | solution.py:15
  27.2 19.7 %all-to-all-start.1 = ((f32[8,32,256]{2,1,0:T(8,128)}), f32[8,32,256]{2,1,0:T(8,128)S(1)}, u32[]{:S(2)}, u32[]{:S(2)}) async-start(f32[8,32,256]{2,1,0:T(8,128)} %bitcast.3), calls=%async_computation.1 | async-start | bytes 524288 | tf_op jit(solution)/shard_map/all_to_all | solution.py:19
  34.2 65.8 %collective-permute-start.6 = (f32[512,512]{1,0:T(8,128)S(1)}, f32[512,512]{1,0:T(8,128)}, u32[]{:S(2)}, u32[]{:S(2)}) collective-permute-start(f32[512,512]{1,0:T(8,128)S(1)} %get-tuple-element.15.refs_4_), channel_id=1, source_target_pairs={{0,32},{32,0},{1,33},{33,1},{2,34},{34,2},{3,35},{35,3},{4,36},{36... | collective-permute-start | bytes 3145736 | tf_op jit(solution)/shard_map/ppermute | solution.py:192
  47.0 53.7 %collective-permute-start.7 = (f32[512,512]{1,0:T(8,128)S(1)}, f32[512,512]{1,0:T(8,128)}, u32[]{:S(2)}, u32[]{:S(2)}) collective-permute-start(f32[512,512]{1,0:T(8,128)S(1)} %collective-permute-done.3.refs_5_), channel_id=1, source_target_pairs={{0,32},{32,0},{1,33},{33,1},{2,34},{34,2},{3,35},{35,3},{4,36},{36... | collective-permute-start | bytes 3145736 | tf_op jit(solution)/shard_map/ppermute | solution.py:192
  48.2 18.5 %all-to-all-start.2 = ((f32[8,2,2048]{2,1,0:T(2,128)}), f32[8,2,2048]{2,1,0:T(2,128)S(1)}, u32[]{:S(2)}, u32[]{:S(2)}) async-start(f32[8,2,2048]{2,1,0:T(2,128)} %bitcast.11), calls=%async_computation.2 | async-start | bytes 262144 | tf_op jit(solution)/shard_map/all_to_all | solution.py:19
  55.1 46.5 %collective-permute-start.8 = (f32[512,512]{1,0:T(8,128)S(1)}, f32[512,512]{1,0:T(8,128)}, u32[]{:S(2)}, u32[]{:S(2)}) collective-permute-start(f32[512,512]{1,0:T(8,128)S(1)} %collective-permute-done.4.refs_6_), channel_id=1, source_target_pairs={{0,32},{32,0},{1,33},{33,1},{2,34},{34,2},{3,35},{35,3},{4,36},{36... | collective-permute-start | bytes 3145736 | tf_op jit(solution)/shard_map/ppermute | solution.py:192
  66.7 34.9 %collective-permute-start.9 = (f32[512,512]{1,0:T(8,128)}, f32[512,512]{1,0:T(8,128)}, u32[]{:S(2)}, u32[]{:S(2)}) collective-permute-start(f32[512,512]{1,0:T(8,128)} %collective-permute-done.5.refs_7_), channel_id=1, source_target_pairs={{0,32},{32,0},{1,33},{33,1},{2,34},{34,2},{3,35},{35,3},{4,36},{36... | collective-permute-start | bytes 3145736 | tf_op jit(solution)/shard_map/ppermute | solution.py:192
  97.0 23.4 %collective-permute-start = (f32[64,2048]{1,0:T(8,128)S(1)}, f32[64,2048]{1,0:T(8,128)S(1)}, u32[]{:S(2)}, u32[]{:S(2)}) collective-permute-start(f32[64,2048]{1,0:T(8,128)S(1)} %bitcast.12), channel_id=1, source_target_pairs={{0,192},{64,0},{128,64},{192,128},{1,193},{65,1},{129,65},{193,129... | collective-permute-start | bytes 1572872 | tf_op jit(solution)/shard_map/ppermute | solution.py:15
  100.0 20.4 %collective-permute-start.1 = (f32[64,2048]{1,0:T(8,128)S(1)}, f32[64,2048]{1,0:T(8,128)S(1)}, u32[]{:S(2)}, u32[]{:S(2)}) collective-permute-start(f32[64,2048]{1,0:T(8,128)S(1)} %bitcast.13), channel_id=1, source_target_pairs={{0,128},{64,192},{128,0},{192,64},{1,129},{65,193},{129,1},{193,65... | collective-permute-start | bytes 1572872 | tf_op jit(solution)/shard_map/ppermute | solution.py:15
  100.7 23.5 %collective-permute-start.2 = (f32[64,2048]{1,0:T(8,128)S(1)}, f32[64,2048]{1,0:T(8,128)S(1)}, u32[]{:S(2)}, u32[]{:S(2)}) collective-permute-start(f32[64,2048]{1,0:T(8,128)S(1)} %bitcast.14), channel_id=1, source_target_pairs={{0,64},{64,128},{128,192},{192,0},{1,65},{65,129},{129,193},{193,1... | collective-permute-start | bytes 1572872 | tf_op jit(solution)/shard_map/ppermute | solution.py:15
  163.0 32.2 %all-to-all-start.5 = ((f32[8,32,1024]{2,1,0:T(8,128)}), f32[8,32,1024]{2,1,0:T(8,128)S(1)}, u32[]{:S(2)}, u32[]{:S(2)}) async-start(f32[8,32,1024]{2,1,0:T(8,128)} %sum_copies.1), calls=%async_computation.5 | async-start | bytes 2097152 | tf_op jit(solution)/shard_map/all_to_all | solution.py:19
  168.3 23.4 %collective-permute-start.10 = (f32[256,512]{1,0:T(8,128)S(1)}, f32[256,512]{1,0:T(8,128)S(1)}, u32[]{:S(2)}, u32[]{:S(2)}) collective-permute-start(f32[256,512]{1,0:T(8,128)S(1)} %get-tuple-element.18), channel_id=1, source_target_pairs={{0,1},{1,2},{2,3},{3,0},{4,5},{5,6},{6,7},{7,4},{8,9},{9,10},{10,1... | collective-permute-start | bytes 1572872 | tf_op jit(solution)/shard_map/ppermute | solution.py:15
  170.6 21.1 %collective-permute-start.11 = (f32[256,512]{1,0:T(8,128)S(1)}, f32[256,512]{1,0:T(8,128)S(1)}, u32[]{:S(2)}, u32[]{:S(2)}) collective-permute-start(f32[256,512]{1,0:T(8,128)S(1)} %get-tuple-element.20), channel_id=1, source_target_pairs={{0,2},{1,3},{2,0},{3,1},{4,6},{5,7},{6,4},{7,5},{8,10},{9,11},{10,... | collective-permute-start | bytes 1572872 | tf_op jit(solution)/shard_map/ppermute | solution.py:15
  170.7 24.4 %collective-permute-start.12 = (f32[256,512]{1,0:T(8,128)S(1)}, f32[256,512]{1,0:T(8,128)S(1)}, u32[]{:S(2)}, u32[]{:S(2)}) collective-permute-start(f32[256,512]{1,0:T(8,128)S(1)} %get-tuple-element.17), channel_id=1, source_target_pairs={{0,3},{1,0},{2,1},{3,2},{4,7},{5,4},{6,5},{7,6},{8,11},{9,8},{10,9... | collective-permute-start | bytes 1572872 | tf_op jit(solution)/shard_map/ppermute | solution.py:15
  172.0 23.3 %collective-permute-start.13 = (f32[256,512]{1,0:T(8,128)S(1)}, f32[256,512]{1,0:T(8,128)}, u32[]{:S(2)}, u32[]{:S(2)}) collective-permute-start(f32[256,512]{1,0:T(8,128)S(1)} %get-tuple-element.19.refs_4_), channel_id=1, source_target_pairs={{0,32},{32,0},{1,33},{33,1},{2,34},{34,2},{3,35},{35,3},{4,36},{36... | collective-permute-start | bytes 1572872 | tf_op jit(solution)/shard_map/ppermute | solution.py:192
  191.7 3.7 %collective-permute-start.14 = (f32[256,512]{1,0:T(8,128)S(1)}, f32[256,512]{1,0:T(8,128)}, u32[]{:S(2)}, u32[]{:S(2)}) collective-permute-start(f32[256,512]{1,0:T(8,128)S(1)} %collective-permute-done.10.refs_5_), channel_id=1, source_target_pairs={{0,32},{32,0},{1,33},{33,1},{2,34},{34,2},{3,35},{35,3},{4,36},{36... | collective-permute-start | bytes 1572872 | tf_op jit(solution)/shard_map/ppermute | solution.py:192
  191.7 3.7 %collective-permute-start.15 = (f32[256,512]{1,0:T(8,128)S(1)}, f32[256,512]{1,0:T(8,128)}, u32[]{:S(2)}, u32[]{:S(2)}) collective-permute-start(f32[256,512]{1,0:T(8,128)S(1)} %collective-permute-done.11.refs_6_), channel_id=1, source_target_pairs={{0,32},{32,0},{1,33},{33,1},{2,34},{34,2},{3,35},{35,3},{4,36},{36... | collective-permute-start | bytes 1572872 | tf_op jit(solution)/shard_map/ppermute | solution.py:192
  195.2 2.0 collective-permute-start.16

commit v5 on v4

--- a/solution.py
+++ b/solution.py
@@ -17,6 +17,11 @@
 
 def pieces_of(array, axis):
     return lax.all_to_all(array, axis, 0, 0)
+
+
+def mirrored_pieces(array, size):
+    groups = [list(range(size)), list(range(2 * size - 1, size - 1, -1))]
+    return lax.all_to_all(array, ("core", "z"), 0, 0, axis_index_groups=groups)
 
 
 def summed_share(array, axis, size):
@@ -212,8 +217,8 @@
     owned = []
     for d in range(ny):
         owned.append(shifted(mine, "y", ny, -d))
-    part = pieces_of(precondition(owned, fisher, nz), "z")
-    whole = pieces_of(sum_copies(part), "z")
+    part = mirrored_pieces(precondition(owned, fisher, nz), nz)
+    whole = mirrored_pieces(sum_copies(part), nz)
     scores = pieces_of(score(split_sides(whole, width), stored, ny, nz), ("y", "x"))
     return jnp.sum(scores, axis=0)
 

time: 223 us -> 225 us (level)
  blocking collectives: 81.3 us -> 78.2 us
  starting transfers between devices: 35.9 us -> 38.6 us
  waiting for transfers between devices: 78.7 us -> 81.1 us
    all_to_all x3 -> x2, blocking collectives: 81.3 us -> 49.3 us  [pieces_of(): return lax.all_to_all(array, axis, 0, 0)]
    all_to_all x0 -> x1, blocking collectives: none -> 28.8 us  [mirrored_pieces(): return lax.all_to_all(array, ('core', 'z'), 0, 0, axis_index_groups=groups)]
    all_to_all x0 -> x1, starting transfers between devices: none -> 6.03 us  [mirrored_pieces(): return lax.all_to_all(array, ('core', 'z'), 0, 0, axis_index_groups=groups)]
    all_to_all x4 -> x3, starting transfers between devices: 23.8 us -> 20.2 us  [pieces_of(): return lax.all_to_all(array, axis, 0, 0)]
    ppermute x9, waiting for transfers between devices: 69.2 us -> 71.6 us  [shifted(): lax.ppermute(array, axis, [(i, (i + steps) % size) for i in range(size)])]
    all_to_all x4 -> x3, waiting for transfers between devices: 7.67 us -> 7.66 us  [pieces_of(): return lax.all_to_all(array, axis, 0, 0)]
where the time goes in v5:
time: 225 us; the launch traced here: 223 us
  waiting for transfers between devices  81.1 us (36%)
  blocking collectives  78.2 us (35%)
  starting transfers between devices  38.6 us (17%)
  Pallas kernels  14.9 us (7%)
  local copies, waits for them, and re-layouts  6.58 us (3%)
  other arithmetic  2.74 us (1%)
    ppermute x9, waiting for transfers between devices, shifted(): lax.ppermute(array, axis, [(i, (i + steps) % size) for i in range(size)])  71.6 us
    all_to_all x2, blocking collectives, pieces_of(): return lax.all_to_all(array, axis, 0, 0)  49.3 us
    all_to_all x1, blocking collectives, mirrored_pieces(): return lax.all_to_all(array, ('core', 'z'), 0, 0, axis_index_groups=groups)  28.8 us
    all_to_all x3, starting transfers between devices, pieces_of(): return lax.all_to_all(array, axis, 0, 0)  20.2 us
    ppermute x9, starting transfers between devices, shifted(): lax.ppermute(array, axis, [(i, (i + steps) % size) for i in range(size)])  11.3 us
    all_to_all x3, waiting for transfers between devices, pieces_of(): return lax.all_to_all(array, axis, 0, 0)  7.66 us
    all_to_all x1, starting transfers between devices, mirrored_pieces(): return lax.all_to_all(array, ('core', 'z'), 0, 0, axis_index_groups=groups)  6.03 us
    pallas_call x1, Pallas kernels, precondition(): pl.pallas_call(kernel, in_specs=[WHOLE] * (count + 2 * nx), out_specs=WHO...  5.95 us
  transfers between devices with their start and end apart: 21, of which 8 were waited for; matrix products, arithmetic and copies ran while one was open for 4% of the time, Pallas kernels for 0%

profile of v5, /device:TPU:6, one launch (start us, length us, event | category | flops | bytes accessed | tf_op | source)
XLA Modules:
  0.0 222.6 jit_solution(16930520502193989433)
XLA Ops:
  0.0 4.3 %project.1 = f32[1024,256]{1,0:T(8,128)} custom-call(bf16[1024,896]{1,0:T(8,128)(2,1)} %bitcast.17, bf16[1024,256]{1,0:T(8,128)(2,1)} %bitcast.18, bf16[896,128]{1,0:T(8,128)(2,1)} %proj_in_ref.1, bf16[256,128]{1,0:T(8,128)(2,1)} %proj_out_ref.1), custom_call_target="tpu_custom_call" | custom-call | tf_op jit(solution)/shard_map/project/pallas_call | solution.py:72
  4.3 6.4 %all-to-all-start = ((f32[4,256,256]{2,1,0:T(8,128)}), f32[4,256,256]{2,1,0:T(8,128)}, u32[]{:S(2)}, u32[]{:S(2)}) async-start(f32[4,256,256]{2,1,0:T(8,128)} %bitcast.16), calls=%async_computation | async-start | bytes 2097152 | tf_op jit(solution)/shard_map/all_to_all | solution.py:19
  10.7 4.0 %constant_dynamic-slice_fusion.4 = (f32[512,512]{1,0:T(8,128)}, f32[512,512]{1,0:T(8,128)}, f32[512,512]{1,0:T(8,128)S(1)}, f32[512,512]{1,0:T(8,128)}) fusion(f32[512,2048]{1,0:T(8,128)} %param.10, s32[]{:T(128)S(6)} %select_n.19, s32[]{:T(128)S(6)} %select_n.17, s32[]{:T(128)S(6)} %select_n.16, s32[]{:T(128)S(6)} %select_n.18), kind=kLoop, calls=%fused_computation.5 | loop fusion | bytes 8388624 | tf_op jit(solution)/shard_map/dynamic_slice | solution.py:194
  14.7 2.9 %collective-permute-start.4 = (f32[512,512]{1,0:T(8,128)}, f32[512,512]{1,0:T(8,128)S(1)}, u32[]{:S(2)}, u32[]{:S(2)}) collective-permute-start(f32[512,512]{1,0:T(8,128)} %get-tuple-element.16), channel_id=1, source_target_pairs={{0,2},{1,3},{2,0},{3,1},{4,6},{5,7},{6,4},{7,5},{8,10},{9,11},{10,... | collective-permute-start | bytes 3145736 | tf_op jit(solution)/shard_map/ppermute | solution.py:15
  17.6 7.7 %all-to-all-done = f32[4,256,256]{2,1,0:T(8,128)} async-done(((f32[4,256,256]{2,1,0:T(8,128)}), f32[4,256,256]{2,1,0:T(8,128)}, u32[]{:S(2)}, u32[]{:S(2)}) %all-to-all-start) | async-done | bytes 1048608 | tf_op jit(solution)/shard_map/all_to_all | solution.py:19
  25.2 2.0 reduce_sum.27
  27.2 6.9 %all-to-all-start.1 = ((f32[8,32,256]{2,1,0:T(8,128)}), f32[8,32,256]{2,1,0:T(8,128)S(1)}, u32[]{:S(2)}, u32[]{:S(2)}) async-start(f32[8,32,256]{2,1,0:T(8,128)} %bitcast.3), calls=%async_computation.1 | async-start | bytes 524288 | tf_op jit(solution)/shard_map/all_to_all | solution.py:19
  34.2 12.8 %collective-permute-done.3.refs_5_ = f32[512,512]{1,0:T(8,128)S(1)} collective-permute-done((f32[512,512]{1,0:T(8,128)}, f32[512,512]{1,0:T(8,128)S(1)}, u32[]{:S(2)}, u32[]{:S(2)}) %collective-permute-start.3) | collective-permute-done | bytes 1048608 | tf_op jit(solution)/shard_map/ppermute | solution.py:15
  48.2 6.9 %all-to-all-start.2 = ((f32[8,2,2048]{2,1,0:T(2,128)}), f32[8,2,2048]{2,1,0:T(2,128)S(1)}, u32[]{:S(2)}, u32[]{:S(2)}) async-start(f32[8,2,2048]{2,1,0:T(2,128)} %bitcast.11), calls=%async_computation.2 | async-start | bytes 262144 | tf_op jit(solution)/shard_map/all_to_all | solution.py:19
  55.4 11.3 %collective-permute-done.5.refs_7_ = f32[512,512]{1,0:T(8,128)} collective-permute-done((f32[512,512]{1,0:T(8,128)}, f32[512,512]{1,0:T(8,128)}, u32[]{:S(2)}, u32[]{:S(2)}) %collective-permute-start.5) | collective-permute-done | bytes 1048608 | tf_op jit(solution)/shard_map/ppermute | solution.py:15
  66.9 30.1 %all_to_all.35 = f32[4,16,2048]{2,1,0:T(8,128)S(1)} all-to-all(f32[4,16,2048]{2,1,0:T(8,128)S(1)} %broadcast_in_dim.8), channel_id=1, replica_groups=mesh['y'=4,'core'=2,'z'=8,'x'=4] {'x'}, dimensions={0} | all-to-all | bytes 1048576 | tf_op jit(solution)/shard_map/all_to_all | solution.py:19
  97.0 3.0 %collective-permute-start = (f32[64,2048]{1,0:T(8,128)S(1)}, f32[64,2048]{1,0:T(8,128)S(1)}, u32[]{:S(2)}, u32[]{:S(2)}) collective-permute-start(f32[64,2048]{1,0:T(8,128)S(1)} %bitcast.12), channel_id=1, source_target_pairs={{0,192},{64,0},{128,64},{192,128},{1,193},{65,1},{129,65},{193,129... | collective-permute-start | bytes 1572872 | tf_op jit(solution)/shard_map/ppermute | solution.py:15
  101.6 18.8 %collective-permute-done.refs_1_ = f32[64,2048]{1,0:T(8,128)S(1)} collective-permute-done((f32[64,2048]{1,0:T(8,128)S(1)}, f32[64,2048]{1,0:T(8,128)S(1)}, u32[]{:S(2)}, u32[]{:S(2)}) %collective-permute-start) | collective-permute-done | bytes 524320 | tf_op jit(solution)/shard_map/ppermute | solution.py:15
  120.4 3.7 %collective-permute-done.2.refs_3_ = f32[64,2048]{1,0:T(8,128)S(1)} collective-permute-done((f32[64,2048]{1,0:T(8,128)S(1)}, f32[64,2048]{1,0:T(8,128)S(1)}, u32[]{:S(2)}, u32[]{:S(2)}) %collective-permute-start.2) | collective-permute-done | bytes 524320 | tf_op jit(solution)/shard_map/ppermute | solution.py:15
  124.1 5.9 %shard_map.64 = f32[8,32,1024]{2,1,0:T(8,128)S(1)} custom-call(f32[64,2048]{1,0:T(8,128)S(1)} %bitcast.15, f32[64,2048]{1,0:T(8,128)S(1)} %collective-permute-done.refs_1_, f32[64,2048]{1,0:T(8,128)S(1)} %collective-permute-done.1.refs_2_, f32[64,2048]{1,0:T(8,128)S(1)} %collective-permute-done.2.refs_3_, f32[512,512]{1,0:T(8,128)S(1)} %get-tuple-element.15.refs_4_, ...), custom_call_target="tpu_custom_call" | custom-call | tf_op jit(solution)/shard_map/pallas_call | solution.py:109
  130.1 28.8 %all_to_all.36.pieces_ref = f32[8,32,1024]{2,1,0:T(8,128)S(1)} all-to-all(f32[8,32,1024]{2,1,0:T(8,128)S(1)} %shard_map.64), channel_id=1, replica_groups={{0,4,8,12,16,20,24,28},{60,56,52,48,44,40,36,32},{1,5,9,13,17,21,25,29}..., dimensions={0} | all-to-all | bytes 2097152 | tf_op jit(solution)/shard_map/all_to_all | solution.py:24
  160.0 6.0 %all-to-all-start.5 = ((f32[8,32,1024]{2,1,0:T(8,128)}), f32[8,32,1024]{2,1,0:T(8,128)S(1)}, u32[]{:S(2)}, u32[]{:S(2)}) async-start(f32[8,32,1024]{2,1,0:T(8,128)} %sum_copies.1), calls=%async_computation.5 | async-start | bytes 2097152 | tf_op jit(solution)/shard_map/all_to_all | solution.py:24
  166.0 1.7 constant_dynamic-slice_fusion
  167.7 2.3 %collective-permute-start.10 = (f32[256,512]{1,0:T(8,128)S(1)}, f32[256,512]{1,0:T(8,128)S(1)}, u32[]{:S(2)}, u32[]{:S(2)}) collective-permute-start(f32[256,512]{1,0:T(8,128)S(1)} %get-tuple-element.18), channel_id=1, source_target_pairs={{0,1},{1,2},{2,3},{3,0},{4,5},{5,6},{6,7},{7,4},{8,9},{9,10},{10,1... | collective-permute-start | bytes 1572872 | tf_op jit(solution)/shard_map/ppermute | solution.py:15
  171.8 21.6 %collective-permute-done.10.refs_5_ = f32[256,512]{1,0:T(8,128)S(1)} collective-permute-done((f32[256,512]{1,0:T(8,128)S(1)}, f32[256,512]{1,0:T(8,128)S(1)}, u32[]{:S(2)}, u32[]{:S(2)}) %collective-permute-start.10) | collective-permute-done | bytes 524320 | tf_op jit(solution)/shard_map/ppermute | solution.py:15
  193.9 3.4 %collective-permute-done.12.refs_7_ = f32[256,512]{1,0:T(8,128)S(1)} collective-permute-done((f32[256,512]{1,0:T(8,128)S(1)}, f32[256,512]{1,0:T(8,128)S(1)}, u32[]{:S(2)}, u32[]{:S(2)}) %collective-permute-start.12) | collective-permute-done | bytes 524320 | tf_op jit(solution)/shard_map/ppermute | solution.py:15
  197.5 1.8 collective-permute-done.16.refs_11_
  199.3 3.4 %score.1 = f32[16,64,256]{2,1,0:T(8,128)S(1)} custom-call(bf16[256,512]{1,0:T(8,128)(2,1)S(1)} %get-tuple-element.9.refs_0_, bf16[256,512]{1,0:T(8,128)(2,1)S(1)} %get-tuple-element.10.refs_1_, bf16[256,512]{1,0:T(8,128)(2,1)S(1)} %get-tuple-element.11.refs_2_, bf16[256,512]{1,0:T(8,128)(2,1)S(1)} %get-tuple-element.12.refs_3_, ...), custom_call_target="tpu_custom_call" | custom-call | tf_op jit(solution)/shard_map/score/pallas_call | solution.py:173
  202.7 19.2 %all_to_all.37 = f32[16,64,256]{2,1,0:T(8,128)S(1)} all-to-all(f32[16,64,256]{2,1,0:T(8,128)S(1)} %score.1), channel_id=1, replica_groups=mesh['y'=4,'core'=2,'z'=8,'x'=4] {'y','x'}, dimensions={0} | all-to-all | bytes 2097152 | tf_op jit(solution)/shard_map/all_to_all | solution.py:19
  (37 shorter events, 7.5 us)
Async XLA Ops:
  4.3 20.9 %all-to-all-start = ((f32[4,256,256]{2,1,0:T(8,128)}), f32[4,256,256]{2,1,0:T(8,128)}, u32[]{:S(2)}, u32[]{:S(2)}) async-start(f32[4,256,256]{2,1,0:T(8,128)} %bitcast.16), calls=%async_computation | async-start | bytes 2097152 | tf_op jit(solution)/shard_map/all_to_all | solution.py:19
  14.6 32.3 %collective-permute-start.3 = (f32[512,512]{1,0:T(8,128)}, f32[512,512]{1,0:T(8,128)S(1)}, u32[]{:S(2)}, u32[]{:S(2)}) collective-permute-start(f32[512,512]{1,0:T(8,128)} %get-tuple-element.14), channel_id=1, source_target_pairs={{0,1},{1,2},{2,3},{3,0},{4,5},{5,6},{6,7},{7,4},{8,9},{9,10},{10,1... | collective-permute-start | bytes 3145736 | tf_op jit(solution)/shard_map/ppermute | solution.py:15
  14.7 40.4 %collective-permute-start.4 = (f32[512,512]{1,0:T(8,128)}, f32[512,512]{1,0:T(8,128)S(1)}, u32[]{:S(2)}, u32[]{:S(2)}) collective-permute-start(f32[512,512]{1,0:T(8,128)} %get-tuple-element.16), channel_id=1, source_target_pairs={{0,2},{1,3},{2,0},{3,1},{4,6},{5,7},{6,4},{7,5},{8,10},{9,11},{10,... | collective-permute-start | bytes 3145736 | tf_op jit(solution)/shard_map/ppermute | solution.py:15
  17.5 49.2 %collective-permute-start.5 = (f32[512,512]{1,0:T(8,128)}, f32[512,512]{1,0:T(8,128)}, u32[]{:S(2)}, u32[]{:S(2)}) collective-permute-start(f32[512,512]{1,0:T(8,128)} %get-tuple-element.13), channel_id=1, source_target_pairs={{0,3},{1,0},{2,1},{3,2},{4,7},{5,4},{6,5},{7,6},{8,11},{9,8},{10,9... | collective-permute-start | bytes 3145736 | tf_op jit(solution)/shard_map/ppermute | solution.py:15
  27.2 19.7 %all-to-all-start.1 = ((f32[8,32,256]{2,1,0:T(8,128)}), f32[8,32,256]{2,1,0:T(8,128)S(1)}, u32[]{:S(2)}, u32[]{:S(2)}) async-start(f32[8,32,256]{2,1,0:T(8,128)} %bitcast.3), calls=%async_computation.1 | async-start | bytes 524288 | tf_op jit(solution)/shard_map/all_to_all | solution.py:19
  34.2 65.8 %collective-permute-start.6 = (f32[512,512]{1,0:T(8,128)S(1)}, f32[512,512]{1,0:T(8,128)}, u32[]{:S(2)}, u32[]{:S(2)}) collective-permute-start(f32[512,512]{1,0:T(8,128)S(1)} %get-tuple-element.15.refs_4_), channel_id=1, source_target_pairs={{0,32},{32,0},{1,33},{33,1},{2,34},{34,2},{3,35},{35,3},{4,36},{36... | collective-permute-start | bytes 3145736 | tf_op jit(solution)/shard_map/ppermute | solution.py:197
  47.0 53.7 %collective-permute-start.7 = (f32[512,512]{1,0:T(8,128)S(1)}, f32[512,512]{1,0:T(8,128)}, u32[]{:S(2)}, u32[]{:S(2)}) collective-permute-start(f32[512,512]{1,0:T(8,128)S(1)} %collective-permute-done.3.refs_5_), channel_id=1, source_target_pairs={{0,32},{32,0},{1,33},{33,1},{2,34},{34,2},{3,35},{35,3},{4,36},{36... | collective-permute-start | bytes 3145736 | tf_op jit(solution)/shard_map/ppermute | solution.py:197
  48.2 18.5 %all-to-all-start.2 = ((f32[8,2,2048]{2,1,0:T(2,128)}), f32[8,2,2048]{2,1,0:T(2,128)S(1)}, u32[]{:S(2)}, u32[]{:S(2)}) async-start(f32[8,2,2048]{2,1,0:T(2,128)} %bitcast.11), calls=%async_computation.2 | async-start | bytes 262144 | tf_op jit(solution)/shard_map/all_to_all | solution.py:19
  55.1 46.5 %collective-permute-start.8 = (f32[512,512]{1,0:T(8,128)S(1)}, f32[512,512]{1,0:T(8,128)}, u32[]{:S(2)}, u32[]{:S(2)}) collective-permute-start(f32[512,512]{1,0:T(8,128)S(1)} %collective-permute-done.4.refs_6_), channel_id=1, source_target_pairs={{0,32},{32,0},{1,33},{33,1},{2,34},{34,2},{3,35},{35,3},{4,36},{36... | collective-permute-start | bytes 3145736 | tf_op jit(solution)/shard_map/ppermute | solution.py:197
  66.7 34.9 %collective-permute-start.9 = (f32[512,512]{1,0:T(8,128)}, f32[512,512]{1,0:T(8,128)}, u32[]{:S(2)}, u32[]{:S(2)}) collective-permute-start(f32[512,512]{1,0:T(8,128)} %collective-permute-done.5.refs_7_), channel_id=1, source_target_pairs={{0,32},{32,0},{1,33},{33,1},{2,34},{34,2},{3,35},{35,3},{4,36},{36... | collective-permute-start | bytes 3145736 | tf_op jit(solution)/shard_map/ppermute | solution.py:197
  97.0 23.4 %collective-permute-start = (f32[64,2048]{1,0:T(8,128)S(1)}, f32[64,2048]{1,0:T(8,128)S(1)}, u32[]{:S(2)}, u32[]{:S(2)}) collective-permute-start(f32[64,2048]{1,0:T(8,128)S(1)} %bitcast.12), channel_id=1, source_target_pairs={{0,192},{64,0},{128,64},{192,128},{1,193},{65,1},{129,65},{193,129... | collective-permute-start | bytes 1572872 | tf_op jit(solution)/shard_map/ppermute | solution.py:15
  100.0 20.4 %collective-permute-start.1 = (f32[64,2048]{1,0:T(8,128)S(1)}, f32[64,2048]{1,0:T(8,128)S(1)}, u32[]{:S(2)}, u32[]{:S(2)}) collective-permute-start(f32[64,2048]{1,0:T(8,128)S(1)} %bitcast.13), channel_id=1, source_target_pairs={{0,128},{64,192},{128,0},{192,64},{1,129},{65,193},{129,1},{193,65... | collective-permute-start | bytes 1572872 | tf_op jit(solution)/shard_map/ppermute | solution.py:15
  100.7 23.5 %collective-permute-start.2 = (f32[64,2048]{1,0:T(8,128)S(1)}, f32[64,2048]{1,0:T(8,128)S(1)}, u32[]{:S(2)}, u32[]{:S(2)}) collective-permute-start(f32[64,2048]{1,0:T(8,128)S(1)} %bitcast.14), channel_id=1, source_target_pairs={{0,64},{64,128},{128,192},{192,0},{1,65},{65,129},{129,193},{193,1... | collective-permute-start | bytes 1572872 | tf_op jit(solution)/shard_map/ppermute | solution.py:15
  160.0 37.3 %all-to-all-start.5 = ((f32[8,32,1024]{2,1,0:T(8,128)}), f32[8,32,1024]{2,1,0:T(8,128)S(1)}, u32[]{:S(2)}, u32[]{:S(2)}) async-start(f32[8,32,1024]{2,1,0:T(8,128)} %sum_copies.1), calls=%async_computation.5 | async-start | bytes 2097152 | tf_op jit(solution)/shard_map/all_to_all | solution.py:24
  167.7 25.6 %collective-permute-start.10 = (f32[256,512]{1,0:T(8,128)S(1)}, f32[256,512]{1,0:T(8,128)S(1)}, u32[]{:S(2)}, u32[]{:S(2)}) collective-permute-start(f32[256,512]{1,0:T(8,128)S(1)} %get-tuple-element.18), channel_id=1, source_target_pairs={{0,1},{1,2},{2,3},{3,0},{4,5},{5,6},{6,7},{7,4},{8,9},{9,10},{10,1... | collective-permute-start | bytes 1572872 | tf_op jit(solution)/shard_map/ppermute | solution.py:15
  170.1 23.7 %collective-permute-start.11 = (f32[256,512]{1,0:T(8,128)S(1)}, f32[256,512]{1,0:T(8,128)S(1)}, u32[]{:S(2)}, u32[]{:S(2)}) collective-permute-start(f32[256,512]{1,0:T(8,128)S(1)} %get-tuple-element.20), channel_id=1, source_target_pairs={{0,2},{1,3},{2,0},{3,1},{4,6},{5,7},{6,4},{7,5},{8,10},{9,11},{10,... | collective-permute-start | bytes 1572872 | tf_op jit(solution)/shard_map/ppermute | solution.py:15
  170.2 27.1 %collective-permute-start.12 = (f32[256,512]{1,0:T(8,128)S(1)}, f32[256,512]{1,0:T(8,128)S(1)}, u32[]{:S(2)}, u32[]{:S(2)}) collective-permute-start(f32[256,512]{1,0:T(8,128)S(1)} %get-tuple-element.17), channel_id=1, source_target_pairs={{0,3},{1,0},{2,1},{3,2},{4,7},{5,4},{6,5},{7,6},{8,11},{9,8},{10,9... | collective-permute-start | bytes 1572872 | tf_op jit(solution)/shard_map/ppermute | solution.py:15
  171.5 26.0 %collective-permute-start.13 = (f32[256,512]{1,0:T(8,128)S(1)}, f32[256,512]{1,0:T(8,128)}, u32[]{:S(2)}, u32[]{:S(2)}) collective-permute-start(f32[256,512]{1,0:T(8,128)S(1)} %get-tuple-element.19.refs_4_), channel_id=1, source_target_pairs={{0,32},{32,0},{1,33},{33,1},{2,34},{34,2},{3,35},{35,3},{4,36},{36... | collective-permute-start | bytes 1572872 | tf_op jit(solution)/shard_map/ppermute | solution.py:197
  193.4 4.1 %collective-permute-start.14 = (f32[256,512]{1,0:T(8,128)S(1)}, f32[256,512]{1,0:T(8,128)}, u32[]{:S(2)}, u32[]{:S(2)}) collective-permute-start(f32[256,512]{1,0:T(8,128)S(1)} %collective-permute-done.10.refs_5_), channel_id=1, source_target_pairs={{0,32},{32,0},{1,33},{33,1},{2,34},{34,2},{3,35},{35,3},{4,36},{36... | collective-permute-start | bytes 1572872 | tf_op jit(solution)/shard_map/ppermute | solution.py:197
  193.8 3.7 %collective-permute-start.15 = (f32[256,512]{1,0:T(8,128)S(1)}, f32[256,512]{1,0:T(8,128)}, u32[]{:S(2)}, u32[]{:S(2)}) collective-permute-start(f32[256,512]{1,0:T(8,128)S(1)} %collective-permute-done.11.refs_6_), channel_id=1, source_target_pairs={{0,32},{32,0},{1,33},{33,1},{2,34},{34,2},{3,35},{35,3},{4,36},{36... | collective-permute-start | bytes 1572872 | tf_op jit(solution)/shard_map/ppermute | solution.py:197
  197.3 2.0 collective-permute-start.16
